TPU v7x, 32 devices: a whole 2x2x4 slice. The times are simulated.
32 devices in a mesh: lat: 8 (over z, core), lon: 4 (over y, x).
Axes of the slice: x: 2, y: 2, z: 4, core: 2. Of those that a mesh axis runs over, the one named last changes fastest.
Arguments:
- misfit: float32 [8, 256, 512], P(None, 'lat', 'lon'), may hold values from -6 to 6
- flow_east: float32 [8, 256, 512], P(None, 'lat', 'lon'), may hold values from -6 to 6
- flow_north: float32 [8, 256, 512], P(None, 'lat', 'lon'), may hold values from -6 to 6
- ocean_depth: float32 [256, 512], P('lat', 'lon'), may hold values from 0.4 to 1.6
- drag_rate: float32 [256, 512], P('lat', 'lon'), may hold values from 0.02 to 0.3
- wet_mask: int32 [256, 512], P('lat', 'lon'), may hold values from 0 to 1, as said below
- legendre: bfloat16 [256, 256, 1024], P(('lon', 'lat')), as said below
- love_factor: float32 [256], replicated, may hold values from 0.2 to 2
- assignment: int32 [256], replicated, may hold values from 0 to 255, as said below
Outputs:
- adjoint_height: float32 [8, 256, 512], P(None, 'lat', 'lon')
- adjoint_east: float32 [8, 256, 512], P(None, 'lat', 'lon')
- adjoint_north: float32 [8, 256, 512], P(None, 'lat', 'lon')
Inputs may be any that keep to these rules, and one draw needn't show every extreme that they name: `wet_mask`: 1 marks a wet cell and 0 land; the first and the last latitude rows are land. `assignment`: A permutation: each of the 256 orders appears once. `legendre`: entry [p, a, n] belongs to degree assignment[p] + n and is zero where assignment[p] + n >= 256.
All inputs are finite; a program needn't handle non-finite values.
Results may differ from a plain program's by a relative error of at most 0.0028.
Values may be sent and summed in bfloat16 or wider, within the bound.
A program may use at most 64 MiB of HBM per device.

v0:
```python
import math

import jax
import jax.numpy as jnp
from jax import lax
from jax.sharding import PartitionSpec as P

TIME_STEPS = 4


TWO_PI = 2.0 * math.pi
exact_mode = lax.Precision.HIGHEST


def with_halo(cells, sides, width):
    for axis, dim in sides:
        count = lax.axis_size(axis)
        head = lax.slice_in_dim(cells, 0, width, axis=dim)
        tail = lax.slice_in_dim(cells, cells.shape[dim] - width, cells.shape[dim], axis=dim)
        cells = jnp.concatenate(
            [
                lax.ppermute(tail, axis, [(i, (i + 1) % count) for i in range(count)]),
                cells,
                lax.ppermute(head, axis, [((i + 1) % count, i) for i in range(count)]),
            ],
            axis=dim,
        )
    return cells


def extend(stacked):
    return with_halo(stacked, (("lat", 2), ("lon", 3)), 1)


def differences(extended):
    east_diff = extended[:, :, 1:-1, 2:] - extended[:, :, 1:-1, :-2]
    north_diff = extended[:, :, 2:, 1:-1] - extended[:, :, :-2, 1:-1]
    return (east_diff, north_diff)


def adjoint_step(height, east_flow, north_flow, wetness, ocean_depth, drag_rate):
    east_diff, north_diff = differences(extend(height[None]))
    retained = 1.0 - drag_rate
    east_flow = wetness * (retained * east_flow - 0.5 * east_diff[0])
    north_flow = wetness * (retained * north_flow - 0.5 * north_diff[0])
    flow_east_diff, flow_north_diff = differences(extend(jnp.stack([east_flow, north_flow])))
    height = wetness * (height - 0.5 * ocean_depth * (flow_east_diff[0] + flow_north_diff[1]))
    return (height, east_flow, north_flow)


def phases(orders, positions, period):
    products = orders[:, None] * positions[None, :] % period
    radians = products.astype(jnp.float32) * (TWO_PI / period)
    return (jnp.cos(radians), jnp.sin(radians))


def spherical(spectra, legendre, weights, lat_count, row_count):
    slot_count = legendre.shape[0]
    degree_count = legendre.shape[2]
    legendre_blocks = legendre.reshape(slot_count, lat_count, row_count, degree_count)
    spectra_blocks = spectra.reshape(slot_count, lat_count, -1, row_count)
    coefficients = jnp.einsum(
        "kicr,kirn->kcn", spectra_blocks, legendre_blocks, preferred_element_type=jnp.float32
    )
    coefficients = (coefficients * weights[:, None, :]).astype(jnp.bfloat16)
    synthesis = jnp.einsum(
        "kcn,kirn->kicr", coefficients, legendre_blocks, preferred_element_type=jnp.float32
    )
    return synthesis.astype(jnp.bfloat16)


def local(
    misfit,
    flow_east,
    flow_north,
    ocean_depth,
    drag_rate,
    wet_mask,
    legendre,
    love_factor,
    assignment,
):
    field_count, row_count, col_count = misfit.shape
    lat_count = lax.axis_size("lat")
    lon_count = lax.axis_size("lon")
    period = col_count * lon_count
    order_count = period // 2
    slot_count = legendre.shape[0]
    degree_count = legendre.shape[2]
    row_pair = row_count // lon_count
    lat_index = lax.axis_index("lat")
    lon_index = lax.axis_index("lon")
    wetness = wet_mask.astype(jnp.float32)
    height = wetness * misfit
    east_flow = wetness * flow_east
    north_flow = wetness * flow_north

    def advance(height, east_flow, north_flow):
        return adjoint_step(height, east_flow, north_flow, wetness, ocean_depth, drag_rate)

    for _ in range(TIME_STEPS):
        height, east_flow, north_flow = advance(height, east_flow, north_flow)
    base = (lon_index * lat_count + lat_index) * slot_count
    my_orders = lax.dynamic_slice_in_dim(assignment, base, slot_count)
    love_pad = jnp.concatenate([love_factor, jnp.zeros((degree_count,), jnp.float32)])
    weights = jax.vmap(
        lambda first_order: lax.dynamic_slice_in_dim(love_pad, first_order, degree_count)
    )(my_orders)
    all_cells = jnp.arange(period, dtype=jnp.int32)
    cos_full, sin_full = phases(assignment, all_cells, period)
    row_block = lax.all_to_all(height, "lon", split_axis=1, concat_axis=2, tiled=True)
    real_part = jnp.einsum("nrx,mx->nrm", row_block, cos_full, precision=exact_mode)
    imag_part = -jnp.einsum("nrx,mx->nrm", row_block, sin_full, precision=exact_mode)
    rowwise = jnp.stack([real_part, imag_part], 2).astype(jnp.bfloat16)
    gathered = rowwise.transpose(3, 2, 0, 1).reshape(lon_count, lat_count, -1)
    received = lax.all_to_all(
        lax.all_to_all(gathered, "lat", split_axis=1, concat_axis=1, tiled=True),
        "lon",
        split_axis=0,
        concat_axis=0,
        tiled=True,
    )
    received = received.reshape(lon_count, lat_count, slot_count, 2, field_count, row_pair)
    spectra = received.transpose(2, 1, 3, 4, 0, 5).reshape(
        slot_count, lat_count, 2 * field_count * row_count
    )
    synthesis = spherical(spectra, legendre, weights, lat_count, row_count)
    arranged = synthesis.reshape(slot_count, lat_count, 2, field_count, lon_count, row_pair)
    arranged = arranged.transpose(4, 1, 0, 2, 3, 5).reshape(lon_count, lat_count, -1)
    returned = lax.all_to_all(
        lax.all_to_all(arranged, "lat", split_axis=1, concat_axis=1, tiled=True),
        "lon",
        split_axis=0,
        concat_axis=0,
        tiled=True,
    )
    returned = returned.reshape(order_count, 2, field_count, row_pair).astype(jnp.float32)
    doubling = jnp.where(assignment == 0, 1.0, 2.0).astype(jnp.float32)
    grid_rows = jnp.einsum(
        "mx,mfr->frx", cos_full * doubling[:, None], returned[:, 0], precision=exact_mode
    ) - jnp.einsum(
        "mx,mfr->frx", sin_full * doubling[:, None], returned[:, 1], precision=exact_mode
    )
    loading = lax.all_to_all(grid_rows, "lon", split_axis=2, concat_axis=1, tiled=True)
    height = height + wetness * loading
    return advance(height, east_flow, north_flow)


def solution(mesh):
    placed = (
        P(None, "lat", "lon"),
        P(None, "lat", "lon"),
        P(None, "lat", "lon"),
        P("lat", "lon"),
        P("lat", "lon"),
        P("lat", "lon"),
        P(("lon", "lat"), None, None),
        P(),
        P(),
    )
    return jax.shard_map(
        local,
        mesh=mesh,
        in_specs=placed,
        out_specs=(P(None, "lat", "lon"), P(None, "lat", "lon"), P(None, "lat", "lon")),
        check_vma=False,
    )
```

profile of v0, /device:TPU:1, one launch (start us, length us, event | category | flops | bytes accessed | tf_op | source)
XLA Modules:
  0.0 250.8 jit_solution(16418631101517796318)
XLA Ops:
  2.4 2.7 %collective-permute-start = (f32[1,8,1,128]{3,1,2,0:T(8,128)S(1)}, f32[1,8,1,128]{3,1,2,0:T(8,128)S(1)}, u32[]{:S(2)}, u32[]{:S(2)}) collective-permute-start(f32[1,8,1,128]{3,1,2,0:T(8,128)S(1)} %get-tuple-element.72), channel_id=1, source_target_pairs={{0,4},{4,8},{8,12},{12,16},{16,20},{20,24},{24,28},{28,0},{1,5},{5... | collective-permute-start | bytes 12296 | tf_op jit(solution)/shard_map/ppermute | solution.py:22
  5.9 2.3 collective-permute-done.1
  8.3 2.4 collective-permute-start.2
  13.3 4.0 %collective-permute-done.3 = f32[1,8,34,1]{3,1,2,0:T(8,128)S(1)} collective-permute-done((f32[1,8,34,1]{3,1,2,0:T(8,128)S(1)}, f32[1,8,34,1]{3,1,2,0:T(8,128)S(1)}, u32[]{:S(2)}, u32[]{:S(2)}) %collective-permute-start.3) | collective-permute-done | bytes 1120 | tf_op jit(solution)/shard_map/ppermute | solution.py:22
  20.5 2.1 collective-permute-done.5
  25.0 3.9 %collective-permute-done.6 = f32[2,8,34,1]{3,1,2,0:T(8,128)S(1)} collective-permute-done((f32[2,8,34,1]{3,1,2,0:T(8,128)S(1)}, f32[2,8,34,1]{3,1,2,0:T(8,128)S(1)}, u32[]{:S(2)}, u32[]{:S(2)}) %collective-permute-start.6) | collective-permute-done | bytes 2208 | tf_op jit(solution)/shard_map/ppermute | solution.py:24
  28.9 6.1 %collective-permute-done.7 = f32[2,8,34,1]{3,1,2,0:T(8,128)S(1)} collective-permute-done((f32[2,8,34,1]{3,1,2,0:T(8,128)S(1)}, f32[2,8,34,1]{3,1,2,0:T(8,128)S(1)}, u32[]{:S(2)}, u32[]{:S(2)}) %collective-permute-start.7) | collective-permute-done | bytes 2208 | tf_op jit(solution)/shard_map/ppermute | solution.py:22
  35.2 2.6 %collective-permute-start.8 = (f32[1,8,1,128]{3,1,2,0:T(8,128)S(1)}, f32[1,8,1,128]{3,1,2,0:T(8,128)S(1)}, u32[]{:S(2)}, u32[]{:S(2)}) collective-permute-start(f32[1,8,1,128]{3,1,2,0:T(8,128)S(1)} %get-tuple-element.70), channel_id=1, source_target_pairs={{0,4},{4,8},{8,12},{12,16},{16,20},{20,24},{24,28},{28,0},{1,5},{5... | collective-permute-start | bytes 12296 | tf_op jit(solution)/shard_map/ppermute | solution.py:22
  38.7 2.2 collective-permute-done.9
  41.0 2.1 collective-permute-start.10
  43.1 2.0 collective-permute-done.10
  45.1 3.8 %collective-permute-done.11 = f32[1,8,34,1]{3,1,2,0:T(8,128)S(1)} collective-permute-done((f32[1,8,34,1]{3,1,2,0:T(8,128)S(1)}, f32[1,8,34,1]{3,1,2,0:T(8,128)S(1)}, u32[]{:S(2)}, u32[]{:S(2)}) %collective-permute-start.11) | collective-permute-done | bytes 1120 | tf_op jit(solution)/shard_map/ppermute | solution.py:22
  55.9 3.9 %collective-permute-done.14 = f32[2,8,34,1]{3,1,2,0:T(8,128)S(1)} collective-permute-done((f32[2,8,34,1]{3,1,2,0:T(8,128)S(1)}, f32[2,8,34,1]{3,1,2,0:T(8,128)S(1)}, u32[]{:S(2)}, u32[]{:S(2)}) %collective-permute-start.14) | collective-permute-done | bytes 2208 | tf_op jit(solution)/shard_map/ppermute | solution.py:24
  59.8 5.9 %collective-permute-done.15 = f32[2,8,34,1]{3,1,2,0:T(8,128)S(1)} collective-permute-done((f32[2,8,34,1]{3,1,2,0:T(8,128)S(1)}, f32[2,8,34,1]{3,1,2,0:T(8,128)S(1)}, u32[]{:S(2)}, u32[]{:S(2)}) %collective-permute-start.15) | collective-permute-done | bytes 2208 | tf_op jit(solution)/shard_map/ppermute | solution.py:22
  65.9 3.3 %collective-permute-start.16 = (f32[1,8,1,128]{3,1,2,0:T(8,128)S(1)}, f32[1,8,1,128]{3,1,2,0:T(8,128)S(1)}, u32[]{:S(2)}, u32[]{:S(2)}) collective-permute-start(f32[1,8,1,128]{3,1,2,0:T(8,128)S(1)} %get-tuple-element.68), channel_id=1, source_target_pairs={{0,4},{4,8},{8,12},{12,16},{16,20},{20,24},{24,28},{28,0},{1,5},{5... | collective-permute-start | bytes 12296 | tf_op jit(solution)/shard_map/ppermute | solution.py:22
  73.9 2.4 collective-permute-done.18
  76.3 2.7 %collective-permute-done.19 = f32[1,8,34,1]{3,1,2,0:T(8,128)S(1)} collective-permute-done((f32[1,8,34,1]{3,1,2,0:T(8,128)S(1)}, f32[1,8,34,1]{3,1,2,0:T(8,128)S(1)}, u32[]{:S(2)}, u32[]{:S(2)}) %collective-permute-start.19) | collective-permute-done | bytes 1120 | tf_op jit(solution)/shard_map/ppermute | solution.py:22
  79.2 2.8 %collective-permute-start.20 = (f32[2,8,1,128]{3,1,2,0:T(8,128)S(1)}, f32[2,8,1,128]{3,1,2,0:T(8,128)S(1)}, u32[]{:S(2)}, u32[]{:S(2)}) collective-permute-start(f32[2,8,1,128]{3,1,2,0:T(8,128)S(1)} %get-tuple-element.41), channel_id=1, source_target_pairs={{0,4},{4,8},{8,12},{12,16},{16,20},{20,24},{24,28},{28,0},{1,5},{5... | collective-permute-start | bytes 24584 | tf_op jit(solution)/shard_map/ppermute | solution.py:22
  86.7 3.9 %collective-permute-done.22 = f32[2,8,34,1]{3,1,2,0:T(8,128)S(1)} collective-permute-done((f32[2,8,34,1]{3,1,2,0:T(8,128)S(1)}, f32[2,8,34,1]{3,1,2,0:T(8,128)S(1)}, u32[]{:S(2)}, u32[]{:S(2)}) %collective-permute-start.22) | collective-permute-done | bytes 2208 | tf_op jit(solution)/shard_map/ppermute | solution.py:24
  90.7 5.8 %collective-permute-done.23 = f32[2,8,34,1]{3,1,2,0:T(8,128)S(1)} collective-permute-done((f32[2,8,34,1]{3,1,2,0:T(8,128)S(1)}, f32[2,8,34,1]{3,1,2,0:T(8,128)S(1)}, u32[]{:S(2)}, u32[]{:S(2)}) %collective-permute-start.23) | collective-permute-done | bytes 2208 | tf_op jit(solution)/shard_map/ppermute | solution.py:22
  96.6 3.0 %collective-permute-start.24 = (f32[1,8,1,128]{3,1,2,0:T(8,128)S(1)}, f32[1,8,1,128]{3,1,2,0:T(8,128)S(1)}, u32[]{:S(2)}, u32[]{:S(2)}) collective-permute-start(f32[1,8,1,128]{3,1,2,0:T(8,128)S(1)} %get-tuple-element.66), channel_id=1, source_target_pairs={{0,4},{4,8},{8,12},{12,16},{16,20},{20,24},{24,28},{28,0},{1,5},{5... | collective-permute-start | bytes 12296 | tf_op jit(solution)/shard_map/ppermute | solution.py:22
  104.3 2.4 collective-permute-done.26
  106.7 2.4 collective-permute-done.27
  109.4 3.5 %collective-permute-start.28 = (f32[2,8,1,128]{3,1,2,0:T(8,128)S(1)}, f32[2,8,1,128]{3,1,2,0:T(8,128)S(1)}, u32[]{:S(2)}, u32[]{:S(2)}) collective-permute-start(f32[2,8,1,128]{3,1,2,0:T(8,128)S(1)} %get-tuple-element.39), channel_id=1, source_target_pairs={{0,4},{4,8},{8,12},{12,16},{16,20},{20,24},{24,28},{28,0},{1,5},{5... | collective-permute-start | bytes 24584 | tf_op jit(solution)/shard_map/ppermute | solution.py:22
  113.9 2.0 collective-permute-done.29
  117.6 4.5 %collective-permute-done.30 = f32[2,8,34,1]{3,1,2,0:T(8,128)S(1)} collective-permute-done((f32[2,8,34,1]{3,1,2,0:T(8,128)S(1)}, f32[2,8,34,1]{3,1,2,0:T(8,128)S(1)}, u32[]{:S(2)}, u32[]{:S(2)}) %collective-permute-start.30) | collective-permute-done | bytes 2208 | tf_op jit(solution)/shard_map/ppermute | solution.py:24
  122.2 5.9 %collective-permute-done.31 = f32[2,8,34,1]{3,1,2,0:T(8,128)S(1)} collective-permute-done((f32[2,8,34,1]{3,1,2,0:T(8,128)S(1)}, f32[2,8,34,1]{3,1,2,0:T(8,128)S(1)}, u32[]{:S(2)}, u32[]{:S(2)}) %collective-permute-start.31) | collective-permute-done | bytes 2208 | tf_op jit(solution)/shard_map/ppermute | solution.py:22
  128.3 6.4 %all_to_all.56 = f32[8,32,128]{2,0,1:T(8,128)S(1)} all-to-all(f32[8,32,128]{2,0,1:T(8,128)S(1)} %fusion.51), channel_id=1, replica_groups=mesh['lat'=8,'lon'=4] {'lon'}, dimensions={1} | all-to-all | bytes 262144 | tf_op jit(solution)/shard_map/all_to_all | solution.py:111
  134.6 2.5 %fusion.5 = bf16[8,8,1,256]{3,1,0,2:T(8,128)(2,1)S(1)} fusion(s32[256]{0:T(256)S(1)} %copy-done.2, f32[8,4,8,128]{3,0,2,1:T(8,128)S(1)} %bitcast.256), kind=kOutput, calls=%fused_computation.11 | convolution fusion | flops 102514688 | bytes 164864 | tf_op jit(solution)/shard_map/nrx,mx->nrm/dot_general | solution.py:112
  137.2 2.5 %fusion.6 = bf16[8,8,1,256]{3,1,0,2:T(8,128)(2,1)S(1)} fusion(s32[256]{0:T(256)S(1)} %copy-done.2, f32[8,4,8,128]{3,0,2,1:T(8,128)S(1)} %bitcast.257), kind=kOutput, calls=%fused_computation.12 | convolution fusion | flops 102531072 | bytes 164864 | tf_op jit(solution)/shard_map/nrx,mx->nrm/dot_general | solution.py:113
  142.8 7.7 %all-to-all-start.1 = ((bf16[4,8,1024]{2,0,1:T(4,128)(2,1)}), bf16[4,8,1024]{2,0,1:T(4,128)(2,1)S(1)}, u32[]{:S(2)}, u32[]{:S(2)}) async-start(bf16[4,8,1024]{2,0,1:T(4,128)(2,1)} %copy.39), calls=%async_computation.1 | async-start | bytes 131072 | tf_op jit(solution)/shard_map/all_to_all | solution.py:117
  150.5 5.1 %all-to-all-done.1 = bf16[4,8,1024]{2,0,1:T(4,128)(2,1)S(1)} async-done(((bf16[4,8,1024]{2,0,1:T(4,128)(2,1)}), bf16[4,8,1024]{2,0,1:T(4,128)(2,1)S(1)}, u32[]{:S(2)}, u32[]{:S(2)}) %all-to-all-start.1) | async-done | bytes 65568 | tf_op jit(solution)/shard_map/all_to_all | solution.py:117
  156.3 3.5 %all-to-all-start.2 = ((bf16[4,8,1024]{2,1,0:T(8,128)(2,1)}), bf16[4,8,1024]{2,1,0:T(8,128)(2,1)S(1)}, u32[]{:S(2)}, u32[]{:S(2)}) async-start(bf16[4,8,1024]{2,1,0:T(8,128)(2,1)} %copy.40), calls=%async_computation.2 | async-start | bytes 131072 | tf_op jit(solution)/shard_map/all_to_all | solution.py:116
  159.9 11.2 %while.1 = (s32[]{:T(128)}, f32[1280]{0:T(1024)S(1)}, s32[8,1]{0,1:T(1,128)S(1)}, f32[8,1024]{1,0:T(8,128)S(1)}, s32[]{:T(128)}, /*index=5*/s32[]{:T(128)}) while((s32[]{:T(128)}, f32[1280]{0:T(1024)S(1)}, s32[8,1]{0,1:T(1,128)S(1)}, f32[8,1024]{1,0:T(8,128)S(1)}, s32[]{:T(128)}, /*index=5*/s32[]{:T(128)}) %tuple.46), condition=%wide.while_cond, body=%wide.while_body.sunk | while | flops 2 | bytes 16473 | solution.py:107
  174.1 7.1 %fusion.3 = bf16[8,8,16,32]{3,2,1,0:T(8,128)(2,1)S(1)} fusion(bf16[8,8,32,1024]{3,2,1,0:T(8,128)(2,1)} %bitcast.210, bf16[8,8,16,32]{3,2,1,0:T(8,128)(2,1)S(1)} %reshape_reshape.3, f32[8,1024]{1,0:T(8,128)S(1)} %get-tuple-element.10), kind=kOutput, calls=%fused_computation.6 | convolution fusion | flops 134512640 | bytes 4358144 | tf_op jit(solution)/shard_map/kcn,kirn->kicr/dot_general | solution.py:66
  183.4 8.3 %all_to_all.57 = bf16[4,8,1024]{2,0,1:T(4,128)(2,1)S(1)} all-to-all(bf16[4,8,1024]{2,0,1:T(4,128)(2,1)S(1)} %copy.43), channel_id=1, replica_groups=mesh['lat'=8,'lon'=4] {'lat'}, dimensions={1} | all-to-all | bytes 131072 | tf_op jit(solution)/shard_map/all_to_all | solution.py:131
  192.3 3.7 %all-to-all-start.4 = ((bf16[4,8,1024]{2,1,0:T(8,128)(2,1)}), bf16[4,8,1024]{2,1,0:T(8,128)(2,1)S(1)}, u32[]{:S(2)}, u32[]{:S(2)}) async-start(bf16[4,8,1024]{2,1,0:T(8,128)(2,1)} %copy.44), calls=%async_computation.4 | async-start | bytes 131072 | tf_op jit(solution)/shard_map/all_to_all | solution.py:130
  196.0 3.7 %all-to-all-done.4 = bf16[4,8,1024]{2,1,0:T(8,128)(2,1)S(1)} async-done(((bf16[4,8,1024]{2,1,0:T(8,128)(2,1)}), bf16[4,8,1024]{2,1,0:T(8,128)(2,1)S(1)}, u32[]{:S(2)}, u32[]{:S(2)}) %all-to-all-start.4) | async-done | bytes 65568 | tf_op jit(solution)/shard_map/all_to_all | solution.py:130
  201.6 2.3 fusion.11
  203.9 2.3 convolution_subtract_fusion
  208.0 6.3 %all_to_all.58 = f32[4,1,8192]{2,1,0:T(1,128)S(1)} all-to-all(f32[4,1,8192]{2,1,0:T(1,128)S(1)} %reshape.81), channel_id=1, replica_groups=mesh['lat'=8,'lon'=4] {'lon'}, dimensions={0} | all-to-all | bytes 262144 | tf_op jit(solution)/shard_map/all_to_all | solution.py:144
  217.6 3.8 %collective-permute-start.32 = (f32[1,8,1,128]{3,1,2,0:T(8,128)S(1)}, f32[1,8,1,128]{3,1,2,0:T(8,128)S(1)}, u32[]{:S(2)}, u32[]{:S(2)}) collective-permute-start(f32[1,8,1,128]{3,1,2,0:T(8,128)S(1)} %get-tuple-element.64), channel_id=1, source_target_pairs={{0,4},{4,8},{8,12},{12,16},{16,20},{20,24},{24,28},{28,0},{1,5},{5... | collective-permute-start | bytes 12296 | tf_op jit(solution)/shard_map/ppermute | solution.py:22
  222.2 2.6 %collective-permute-done.33 = f32[1,8,1,128]{3,1,2,0:T(8,128)S(1)} collective-permute-done((f32[1,8,1,128]{3,1,2,0:T(8,128)S(1)}, f32[1,8,1,128]{3,1,2,0:T(8,128)S(1)}, u32[]{:S(2)}, u32[]{:S(2)}) %collective-permute-start.33) | collective-permute-done | bytes 4128 | tf_op jit(solution)/shard_map/ppermute | solution.py:24
  226.4 2.4 collective-permute-done.34
  228.8 3.2 %collective-permute-done.35 = f32[1,8,34,1]{3,1,2,0:T(8,128)S(1)} collective-permute-done((f32[1,8,34,1]{3,1,2,0:T(8,128)S(1)}, f32[1,8,34,1]{3,1,2,0:T(8,128)S(1)}, u32[]{:S(2)}, u32[]{:S(2)}) %collective-permute-start.35) | collective-permute-done | bytes 1120 | tf_op jit(solution)/shard_map/ppermute | solution.py:22
  235.2 2.0 collective-permute-done.37
  240.3 3.2 %collective-permute-done.38 = f32[2,8,34,1]{3,1,2,0:T(8,128)S(1)} collective-permute-done((f32[2,8,34,1]{3,1,2,0:T(8,128)S(1)}, f32[2,8,34,1]{3,1,2,0:T(8,128)S(1)}, u32[]{:S(2)}, u32[]{:S(2)}) %collective-permute-start.38) | collective-permute-done | bytes 2208 | tf_op jit(solution)/shard_map/ppermute | solution.py:24
  243.5 6.5 %collective-permute-done.39 = f32[2,8,34,1]{3,1,2,0:T(8,128)S(1)} collective-permute-done((f32[2,8,34,1]{3,1,2,0:T(8,128)S(1)}, f32[2,8,34,1]{3,1,2,0:T(8,128)S(1)}, u32[]{:S(2)}, u32[]{:S(2)}) %collective-permute-start.39) | collective-permute-done | bytes 2208 | tf_op jit(solution)/shard_map/ppermute | solution.py:22
  (154 shorter events, 73.9 us)
Async XLA Ops:
  0.6 34.4 %copy-start = (f32[8,32,128]{2,1,0:T(8,128)S(1)}, f32[8,32,128]{2,1,0:T(8,128)}, u32[]{:S(2)}) copy-start(f32[8,32,128]{2,1,0:T(8,128)} %param.9) | copy-start | bytes 393220
  2.4 3.5 %collective-permute-start = (f32[1,8,1,128]{3,1,2,0:T(8,128)S(1)}, f32[1,8,1,128]{3,1,2,0:T(8,128)S(1)}, u32[]{:S(2)}, u32[]{:S(2)}) collective-permute-start(f32[1,8,1,128]{3,1,2,0:T(8,128)S(1)} %get-tuple-element.72), channel_id=1, source_target_pairs={{0,4},{4,8},{8,12},{12,16},{16,20},{20,24},{24,28},{28,0},{1,5},{5... | collective-permute-start | bytes 12296 | tf_op jit(solution)/shard_map/ppermute | solution.py:22
  5.1 3.0 %collective-permute-start.1 = (f32[1,8,1,128]{3,1,2,0:T(8,128)S(1)}, f32[1,8,1,128]{3,1,2,0:T(8,128)S(1)}, u32[]{:S(2)}, u32[]{:S(2)}) collective-permute-start(f32[1,8,1,128]{3,1,2,0:T(8,128)S(1)} %get-tuple-element.71), channel_id=1, source_target_pairs={{4,0},{8,4},{12,8},{16,12},{20,16},{24,20},{28,24},{0,28},{5,1},{9... | collective-permute-start | bytes 12296 | tf_op jit(solution)/shard_map/ppermute | solution.py:24
  8.3 5.1 %collective-permute-start.2 = (f32[1,8,34,1]{3,1,2,0:T(8,128)S(1)}, f32[1,8,34,1]{3,1,2,0:T(8,128)S(1)}, u32[]{:S(2)}, u32[]{:S(2)}) collective-permute-start(f32[1,8,34,1]{3,1,2,0:T(8,128)S(1)} %get-tuple-element.61), channel_id=1, source_target_pairs={{1,0},{2,1},{3,2},{0,3},{5,4},{6,5},{7,6},{4,7},{9,8},{10,9},{11,1... | collective-permute-start | bytes 3272 | tf_op jit(solution)/shard_map/ppermute | solution.py:24
  10.7 6.6 %collective-permute-start.3 = (f32[1,8,34,1]{3,1,2,0:T(8,128)S(1)}, f32[1,8,34,1]{3,1,2,0:T(8,128)S(1)}, u32[]{:S(2)}, u32[]{:S(2)}) collective-permute-start(f32[1,8,34,1]{3,1,2,0:T(8,128)S(1)} %get-tuple-element.62), channel_id=1, source_target_pairs={{0,1},{1,2},{2,3},{3,0},{4,5},{5,6},{6,7},{7,4},{8,9},{9,10},{10,1... | collective-permute-start | bytes 3272 | tf_op jit(solution)/shard_map/ppermute | solution.py:22
  18.5 2.0 collective-permute-start.4
  19.5 3.1 %collective-permute-start.5 = (f32[2,8,1,128]{3,1,2,0:T(8,128)S(1)}, f32[2,8,1,128]{3,1,2,0:T(8,128)S(1)}, u32[]{:S(2)}, u32[]{:S(2)}) collective-permute-start(f32[2,8,1,128]{3,1,2,0:T(8,128)S(1)} %get-tuple-element.46), channel_id=1, source_target_pairs={{4,0},{8,4},{12,8},{16,12},{20,16},{24,20},{28,24},{0,28},{5,1},{9... | collective-permute-start | bytes 24584 | tf_op jit(solution)/shard_map/ppermute | solution.py:24
  22.8 6.1 %collective-permute-start.6 = (f32[2,8,34,1]{3,1,2,0:T(8,128)S(1)}, f32[2,8,34,1]{3,1,2,0:T(8,128)S(1)}, u32[]{:S(2)}, u32[]{:S(2)}) collective-permute-start(f32[2,8,34,1]{3,1,2,0:T(8,128)S(1)} %get-tuple-element.36), channel_id=1, source_target_pairs={{1,0},{2,1},{3,2},{0,3},{5,4},{6,5},{7,6},{4,7},{9,8},{10,9},{11,1... | collective-permute-start | bytes 6536 | tf_op jit(solution)/shard_map/ppermute | solution.py:24
  23.9 11.1 %collective-permute-start.7 = (f32[2,8,34,1]{3,1,2,0:T(8,128)S(1)}, f32[2,8,34,1]{3,1,2,0:T(8,128)S(1)}, u32[]{:S(2)}, u32[]{:S(2)}) collective-permute-start(f32[2,8,34,1]{3,1,2,0:T(8,128)S(1)} %get-tuple-element.35), channel_id=1, source_target_pairs={{0,1},{1,2},{2,3},{3,0},{4,5},{5,6},{6,7},{7,4},{8,9},{9,10},{10,1... | collective-permute-start | bytes 6536 | tf_op jit(solution)/shard_map/ppermute | solution.py:22
  35.2 3.5 %collective-permute-start.8 = (f32[1,8,1,128]{3,1,2,0:T(8,128)S(1)}, f32[1,8,1,128]{3,1,2,0:T(8,128)S(1)}, u32[]{:S(2)}, u32[]{:S(2)}) collective-permute-start(f32[1,8,1,128]{3,1,2,0:T(8,128)S(1)} %get-tuple-element.70), channel_id=1, source_target_pairs={{0,4},{4,8},{8,12},{12,16},{16,20},{20,24},{24,28},{28,0},{1,5},{5... | collective-permute-start | bytes 12296 | tf_op jit(solution)/shard_map/ppermute | solution.py:22
  37.8 3.0 %collective-permute-start.9 = (f32[1,8,1,128]{3,1,2,0:T(8,128)S(1)}, f32[1,8,1,128]{3,1,2,0:T(8,128)S(1)}, u32[]{:S(2)}, u32[]{:S(2)}) collective-permute-start(f32[1,8,1,128]{3,1,2,0:T(8,128)S(1)} %get-tuple-element.69), channel_id=1, source_target_pairs={{4,0},{8,4},{12,8},{16,12},{20,16},{24,20},{28,24},{0,28},{5,1},{9... | collective-permute-start | bytes 12296 | tf_op jit(solution)/shard_map/ppermute | solution.py:24
  41.0 4.2 %collective-permute-start.10 = (f32[1,8,34,1]{3,1,2,0:T(8,128)S(1)}, f32[1,8,34,1]{3,1,2,0:T(8,128)S(1)}, u32[]{:S(2)}, u32[]{:S(2)}) collective-permute-start(f32[1,8,34,1]{3,1,2,0:T(8,128)S(1)} %get-tuple-element.59), channel_id=1, source_target_pairs={{1,0},{2,1},{3,2},{0,3},{5,4},{6,5},{7,6},{4,7},{9,8},{10,9},{11,1... | collective-permute-start | bytes 3272 | tf_op jit(solution)/shard_map/ppermute | solution.py:24
  43.1 5.8 %collective-permute-start.11 = (f32[1,8,34,1]{3,1,2,0:T(8,128)S(1)}, f32[1,8,34,1]{3,1,2,0:T(8,128)S(1)}, u32[]{:S(2)}, u32[]{:S(2)}) collective-permute-start(f32[1,8,34,1]{3,1,2,0:T(8,128)S(1)} %get-tuple-element.60), channel_id=1, source_target_pairs={{0,1},{1,2},{2,3},{3,0},{4,5},{5,6},{6,7},{7,4},{8,9},{9,10},{10,1... | collective-permute-start | bytes 3272 | tf_op jit(solution)/shard_map/ppermute | solution.py:22
  49.1 3.4 %collective-permute-start.12 = (f32[2,8,1,128]{3,1,2,0:T(8,128)S(1)}, f32[2,8,1,128]{3,1,2,0:T(8,128)S(1)}, u32[]{:S(2)}, u32[]{:S(2)}) collective-permute-start(f32[2,8,1,128]{3,1,2,0:T(8,128)S(1)} %get-tuple-element.43), channel_id=1, source_target_pairs={{0,4},{4,8},{8,12},{12,16},{16,20},{20,24},{24,28},{28,0},{1,5},{5... | collective-permute-start | bytes 24584 | tf_op jit(solution)/shard_map/ppermute | solution.py:22
  51.1 3.1 %collective-permute-start.13 = (f32[2,8,1,128]{3,1,2,0:T(8,128)S(1)}, f32[2,8,1,128]{3,1,2,0:T(8,128)S(1)}, u32[]{:S(2)}, u32[]{:S(2)}) collective-permute-start(f32[2,8,1,128]{3,1,2,0:T(8,128)S(1)} %get-tuple-element.44), channel_id=1, source_target_pairs={{4,0},{8,4},{12,8},{16,12},{20,16},{24,20},{28,24},{0,28},{5,1},{9... | collective-permute-start | bytes 24584 | tf_op jit(solution)/shard_map/ppermute | solution.py:24
  54.4 5.5 %collective-permute-start.14 = (f32[2,8,34,1]{3,1,2,0:T(8,128)S(1)}, f32[2,8,34,1]{3,1,2,0:T(8,128)S(1)}, u32[]{:S(2)}, u32[]{:S(2)}) collective-permute-start(f32[2,8,34,1]{3,1,2,0:T(8,128)S(1)} %get-tuple-element.34), channel_id=1, source_target_pairs={{1,0},{2,1},{3,2},{0,3},{5,4},{6,5},{7,6},{4,7},{9,8},{10,9},{11,1... | collective-permute-start | bytes 6536 | tf_op jit(solution)/shard_map/ppermute | solution.py:24
  55.0 10.7 %collective-permute-start.15 = (f32[2,8,34,1]{3,1,2,0:T(8,128)S(1)}, f32[2,8,34,1]{3,1,2,0:T(8,128)S(1)}, u32[]{:S(2)}, u32[]{:S(2)}) collective-permute-start(f32[2,8,34,1]{3,1,2,0:T(8,128)S(1)} %get-tuple-element.33), channel_id=1, source_target_pairs={{0,1},{1,2},{2,3},{3,0},{4,5},{5,6},{6,7},{7,4},{8,9},{9,10},{10,1... | collective-permute-start | bytes 6536 | tf_op jit(solution)/shard_map/ppermute | solution.py:22
  65.9 4.4 %collective-permute-start.16 = (f32[1,8,1,128]{3,1,2,0:T(8,128)S(1)}, f32[1,8,1,128]{3,1,2,0:T(8,128)S(1)}, u32[]{:S(2)}, u32[]{:S(2)}) collective-permute-start(f32[1,8,1,128]{3,1,2,0:T(8,128)S(1)} %get-tuple-element.68), channel_id=1, source_target_pairs={{0,4},{4,8},{8,12},{12,16},{16,20},{20,24},{24,28},{28,0},{1,5},{5... | collective-permute-start | bytes 12296 | tf_op jit(solution)/shard_map/ppermute | solution.py:22
  69.2 3.0 %collective-permute-start.17 = (f32[1,8,1,128]{3,1,2,0:T(8,128)S(1)}, f32[1,8,1,128]{3,1,2,0:T(8,128)S(1)}, u32[]{:S(2)}, u32[]{:S(2)}) collective-permute-start(f32[1,8,1,128]{3,1,2,0:T(8,128)S(1)} %get-tuple-element.67), channel_id=1, source_target_pairs={{4,0},{8,4},{12,8},{16,12},{20,16},{24,20},{28,24},{0,28},{5,1},{9... | collective-permute-start | bytes 12296 | tf_op jit(solution)/shard_map/ppermute | solution.py:24
  72.3 4.0 %collective-permute-start.18 = (f32[1,8,34,1]{3,1,2,0:T(8,128)S(1)}, f32[1,8,34,1]{3,1,2,0:T(8,128)S(1)}, u32[]{:S(2)}, u32[]{:S(2)}) collective-permute-start(f32[1,8,34,1]{3,1,2,0:T(8,128)S(1)} %get-tuple-element.57), channel_id=1, source_target_pairs={{1,0},{2,1},{3,2},{0,3},{5,4},{6,5},{7,6},{4,7},{9,8},{10,9},{11,1... | collective-permute-start | bytes 3272 | tf_op jit(solution)/shard_map/ppermute | solution.py:24
  73.5 5.5 %collective-permute-start.19 = (f32[1,8,34,1]{3,1,2,0:T(8,128)S(1)}, f32[1,8,34,1]{3,1,2,0:T(8,128)S(1)}, u32[]{:S(2)}, u32[]{:S(2)}) collective-permute-start(f32[1,8,34,1]{3,1,2,0:T(8,128)S(1)} %get-tuple-element.58), channel_id=1, source_target_pairs={{0,1},{1,2},{2,3},{3,0},{4,5},{5,6},{6,7},{7,4},{8,9},{9,10},{10,1... | collective-permute-start | bytes 3272 | tf_op jit(solution)/shard_map/ppermute | solution.py:22
  79.2 55.5 %copy-start.2 = (s32[256]{0:T(256)S(1)}, s32[256]{0:T(256)}, u32[]{:S(2)}) copy-start(s32[256]{0:T(256)} %param.17) | copy-start | bytes 3076
  79.2 4.3 %collective-permute-start.20 = (f32[2,8,1,128]{3,1,2,0:T(8,128)S(1)}, f32[2,8,1,128]{3,1,2,0:T(8,128)S(1)}, u32[]{:S(2)}, u32[]{:S(2)}) collective-permute-start(f32[2,8,1,128]{3,1,2,0:T(8,128)S(1)} %get-tuple-element.41), channel_id=1, source_target_pairs={{0,4},{4,8},{8,12},{12,16},{16,20},{20,24},{24,28},{28,0},{1,5},{5... | collective-permute-start | bytes 24584 | tf_op jit(solution)/shard_map/ppermute | solution.py:22
  82.0 3.1 %collective-permute-start.21 = (f32[2,8,1,128]{3,1,2,0:T(8,128)S(1)}, f32[2,8,1,128]{3,1,2,0:T(8,128)S(1)}, u32[]{:S(2)}, u32[]{:S(2)}) collective-permute-start(f32[2,8,1,128]{3,1,2,0:T(8,128)S(1)} %get-tuple-element.42), channel_id=1, source_target_pairs={{4,0},{8,4},{12,8},{16,12},{20,16},{24,20},{28,24},{0,28},{5,1},{9... | collective-permute-start | bytes 24584 | tf_op jit(solution)/shard_map/ppermute | solution.py:24
  85.2 5.5 %collective-permute-start.22 = (f32[2,8,34,1]{3,1,2,0:T(8,128)S(1)}, f32[2,8,34,1]{3,1,2,0:T(8,128)S(1)}, u32[]{:S(2)}, u32[]{:S(2)}) collective-permute-start(f32[2,8,34,1]{3,1,2,0:T(8,128)S(1)} %get-tuple-element.32), channel_id=1, source_target_pairs={{1,0},{2,1},{3,2},{0,3},{5,4},{6,5},{7,6},{4,7},{9,8},{10,9},{11,1... | collective-permute-start | bytes 6536 | tf_op jit(solution)/shard_map/ppermute | solution.py:24
  85.3 11.1 %collective-permute-start.23 = (f32[2,8,34,1]{3,1,2,0:T(8,128)S(1)}, f32[2,8,34,1]{3,1,2,0:T(8,128)S(1)}, u32[]{:S(2)}, u32[]{:S(2)}) collective-permute-start(f32[2,8,34,1]{3,1,2,0:T(8,128)S(1)} %get-tuple-element.31), channel_id=1, source_target_pairs={{0,1},{1,2},{2,3},{3,0},{4,5},{5,6},{6,7},{7,4},{8,9},{9,10},{10,1... | collective-permute-start | bytes 6536 | tf_op jit(solution)/shard_map/ppermute | solution.py:22
  96.6 4.5 %collective-permute-start.24 = (f32[1,8,1,128]{3,1,2,0:T(8,128)S(1)}, f32[1,8,1,128]{3,1,2,0:T(8,128)S(1)}, u32[]{:S(2)}, u32[]{:S(2)}) collective-permute-start(f32[1,8,1,128]{3,1,2,0:T(8,128)S(1)} %get-tuple-element.66), channel_id=1, source_target_pairs={{0,4},{4,8},{8,12},{12,16},{16,20},{20,24},{24,28},{28,0},{1,5},{5... | collective-permute-start | bytes 12296 | tf_op jit(solution)/shard_map/ppermute | solution.py:22
  99.6 3.0 %collective-permute-start.25 = (f32[1,8,1,128]{3,1,2,0:T(8,128)S(1)}, f32[1,8,1,128]{3,1,2,0:T(8,128)S(1)}, u32[]{:S(2)}, u32[]{:S(2)}) collective-permute-start(f32[1,8,1,128]{3,1,2,0:T(8,128)S(1)} %get-tuple-element.65), channel_id=1, source_target_pairs={{4,0},{8,4},{12,8},{16,12},{20,16},{24,20},{28,24},{0,28},{5,1},{9... | collective-permute-start | bytes 12296 | tf_op jit(solution)/shard_map/ppermute | solution.py:24
  102.8 4.0 %collective-permute-start.26 = (f32[1,8,34,1]{3,1,2,0:T(8,128)S(1)}, f32[1,8,34,1]{3,1,2,0:T(8,128)S(1)}, u32[]{:S(2)}, u32[]{:S(2)}) collective-permute-start(f32[1,8,34,1]{3,1,2,0:T(8,128)S(1)} %get-tuple-element.55), channel_id=1, source_target_pairs={{1,0},{2,1},{3,2},{0,3},{5,4},{6,5},{7,6},{4,7},{9,8},{10,9},{11,1... | collective-permute-start | bytes 3272 | tf_op jit(solution)/shard_map/ppermute | solution.py:24
  104.3 4.9 %collective-permute-start.27 = (f32[1,8,34,1]{3,1,2,0:T(8,128)S(1)}, f32[1,8,34,1]{3,1,2,0:T(8,128)S(1)}, u32[]{:S(2)}, u32[]{:S(2)}) collective-permute-start(f32[1,8,34,1]{3,1,2,0:T(8,128)S(1)} %get-tuple-element.56), channel_id=1, source_target_pairs={{0,1},{1,2},{2,3},{3,0},{4,5},{5,6},{6,7},{7,4},{8,9},{9,10},{10,1... | collective-permute-start | bytes 3272 | tf_op jit(solution)/shard_map/ppermute | solution.py:22
  109.4 4.6 %collective-permute-start.28 = (f32[2,8,1,128]{3,1,2,0:T(8,128)S(1)}, f32[2,8,1,128]{3,1,2,0:T(8,128)S(1)}, u32[]{:S(2)}, u32[]{:S(2)}) collective-permute-start(f32[2,8,1,128]{3,1,2,0:T(8,128)S(1)} %get-tuple-element.39), channel_id=1, source_target_pairs={{0,4},{4,8},{8,12},{12,16},{16,20},{20,24},{24,28},{28,0},{1,5},{5... | collective-permute-start | bytes 24584 | tf_op jit(solution)/shard_map/ppermute | solution.py:22
  112.9 3.1 %collective-permute-start.29 = (f32[2,8,1,128]{3,1,2,0:T(8,128)S(1)}, f32[2,8,1,128]{3,1,2,0:T(8,128)S(1)}, u32[]{:S(2)}, u32[]{:S(2)}) collective-permute-start(f32[2,8,1,128]{3,1,2,0:T(8,128)S(1)} %get-tuple-element.40), channel_id=1, source_target_pairs={{4,0},{8,4},{12,8},{16,12},{20,16},{24,20},{28,24},{0,28},{5,1},{9... | collective-permute-start | bytes 24584 | tf_op jit(solution)/shard_map/ppermute | solution.py:24
  116.1 6.1 %collective-permute-start.30 = (f32[2,8,34,1]{3,1,2,0:T(8,128)S(1)}, f32[2,8,34,1]{3,1,2,0:T(8,128)S(1)}, u32[]{:S(2)}, u32[]{:S(2)}) collective-permute-start(f32[2,8,34,1]{3,1,2,0:T(8,128)S(1)} %get-tuple-element.30), channel_id=1, source_target_pairs={{1,0},{2,1},{3,2},{0,3},{5,4},{6,5},{7,6},{4,7},{9,8},{10,9},{11,1... | collective-permute-start | bytes 6536 | tf_op jit(solution)/shard_map/ppermute | solution.py:24
  116.5 43.3 %copy-start.1 = (f32[256]{0:T(256)S(1)}, f32[256]{0:T(256)}, u32[]{:S(2)}) copy-start(f32[256]{0:T(256)} %param.16) | copy-start | bytes 3076
  116.5 11.6 %collective-permute-start.31 = (f32[2,8,34,1]{3,1,2,0:T(8,128)S(1)}, f32[2,8,34,1]{3,1,2,0:T(8,128)S(1)}, u32[]{:S(2)}, u32[]{:S(2)}) collective-permute-start(f32[2,8,34,1]{3,1,2,0:T(8,128)S(1)} %get-tuple-element.29), channel_id=1, source_target_pairs={{0,1},{1,2},{2,3},{3,0},{4,5},{5,6},{6,7},{7,4},{8,9},{9,10},{10,1... | collective-permute-start | bytes 6536 | tf_op jit(solution)/shard_map/ppermute | solution.py:22
  142.8 12.8 %all-to-all-start.1 = ((bf16[4,8,1024]{2,0,1:T(4,128)(2,1)}), bf16[4,8,1024]{2,0,1:T(4,128)(2,1)S(1)}, u32[]{:S(2)}, u32[]{:S(2)}) async-start(bf16[4,8,1024]{2,0,1:T(4,128)(2,1)} %copy.39), calls=%async_computation.1 | async-start | bytes 131072 | tf_op jit(solution)/shard_map/all_to_all | solution.py:117
  156.3 14.8 %all-to-all-start.2 = ((bf16[4,8,1024]{2,1,0:T(8,128)(2,1)}), bf16[4,8,1024]{2,1,0:T(8,128)(2,1)S(1)}, u32[]{:S(2)}, u32[]{:S(2)}) async-start(bf16[4,8,1024]{2,1,0:T(8,128)(2,1)} %copy.40), calls=%async_computation.2 | async-start | bytes 131072 | tf_op jit(solution)/shard_map/all_to_all | solution.py:116
  192.3 7.3 %all-to-all-start.4 = ((bf16[4,8,1024]{2,1,0:T(8,128)(2,1)}), bf16[4,8,1024]{2,1,0:T(8,128)(2,1)S(1)}, u32[]{:S(2)}, u32[]{:S(2)}) async-start(bf16[4,8,1024]{2,1,0:T(8,128)(2,1)} %copy.44), calls=%async_computation.4 | async-start | bytes 131072 | tf_op jit(solution)/shard_map/all_to_all | solution.py:130
  217.6 4.6 %collective-permute-start.32 = (f32[1,8,1,128]{3,1,2,0:T(8,128)S(1)}, f32[1,8,1,128]{3,1,2,0:T(8,128)S(1)}, u32[]{:S(2)}, u32[]{:S(2)}) collective-permute-start(f32[1,8,1,128]{3,1,2,0:T(8,128)S(1)} %get-tuple-element.64), channel_id=1, source_target_pairs={{0,4},{4,8},{8,12},{12,16},{16,20},{20,24},{24,28},{28,0},{1,5},{5... | collective-permute-start | bytes 12296 | tf_op jit(solution)/shard_map/ppermute | solution.py:22
  221.4 3.3 %collective-permute-start.33 = (f32[1,8,1,128]{3,1,2,0:T(8,128)S(1)}, f32[1,8,1,128]{3,1,2,0:T(8,128)S(1)}, u32[]{:S(2)}, u32[]{:S(2)}) collective-permute-start(f32[1,8,1,128]{3,1,2,0:T(8,128)S(1)} %get-tuple-element.63), channel_id=1, source_target_pairs={{4,0},{8,4},{12,8},{16,12},{20,16},{24,20},{28,24},{0,28},{5,1},{9... | collective-permute-start | bytes 12296 | tf_op jit(solution)/shard_map/ppermute | solution.py:24
  224.9 4.0 %collective-permute-start.34 = (f32[1,8,34,1]{3,1,2,0:T(8,128)S(1)}, f32[1,8,34,1]{3,1,2,0:T(8,128)S(1)}, u32[]{:S(2)}, u32[]{:S(2)}) collective-permute-start(f32[1,8,34,1]{3,1,2,0:T(8,128)S(1)} %get-tuple-element.53), channel_id=1, source_target_pairs={{1,0},{2,1},{3,2},{0,3},{5,4},{6,5},{7,6},{4,7},{9,8},{10,9},{11,1... | collective-permute-start | bytes 3272 | tf_op jit(solution)/shard_map/ppermute | solution.py:24
  225.3 6.6 %collective-permute-start.35 = (f32[1,8,34,1]{3,1,2,0:T(8,128)S(1)}, f32[1,8,34,1]{3,1,2,0:T(8,128)S(1)}, u32[]{:S(2)}, u32[]{:S(2)}) collective-permute-start(f32[1,8,34,1]{3,1,2,0:T(8,128)S(1)} %get-tuple-element.54), channel_id=1, source_target_pairs={{0,1},{1,2},{2,3},{3,0},{4,5},{5,6},{6,7},{7,4},{8,9},{9,10},{10,1... | collective-permute-start | bytes 3272 | tf_op jit(solution)/shard_map/ppermute | solution.py:22
  232.2 3.1 %collective-permute-start.36 = (f32[2,8,1,128]{3,1,2,0:T(8,128)S(1)}, f32[2,8,1,128]{3,1,2,0:T(8,128)S(1)}, u32[]{:S(2)}, u32[]{:S(2)}) collective-permute-start(f32[2,8,1,128]{3,1,2,0:T(8,128)S(1)} %get-tuple-element.37), channel_id=1, source_target_pairs={{0,4},{4,8},{8,12},{12,16},{16,20},{20,24},{24,28},{28,0},{1,5},{5... | collective-permute-start | bytes 24584 | tf_op jit(solution)/shard_map/ppermute | solution.py:22
  234.2 3.1 %collective-permute-start.37 = (f32[2,8,1,128]{3,1,2,0:T(8,128)S(1)}, f32[2,8,1,128]{3,1,2,0:T(8,128)S(1)}, u32[]{:S(2)}, u32[]{:S(2)}) collective-permute-start(f32[2,8,1,128]{3,1,2,0:T(8,128)S(1)} %get-tuple-element.38), channel_id=1, source_target_pairs={{4,0},{8,4},{12,8},{16,12},{20,16},{24,20},{28,24},{0,28},{5,1},{9... | collective-permute-start | bytes 24584 | tf_op jit(solution)/shard_map/ppermute | solution.py:24
  237.4 6.0 %collective-permute-start.38 = (f32[2,8,34,1]{3,1,2,0:T(8,128)S(1)}, f32[2,8,34,1]{3,1,2,0:T(8,128)S(1)}, u32[]{:S(2)}, u32[]{:S(2)}) collective-permute-start(f32[2,8,34,1]{3,1,2,0:T(8,128)S(1)} %get-tuple-element.28), channel_id=1, source_target_pairs={{1,0},{2,1},{3,2},{0,3},{5,4},{6,5},{7,6},{4,7},{9,8},{10,9},{11,1... | collective-permute-start | bytes 6536 | tf_op jit(solution)/shard_map/ppermute | solution.py:24
  238.7 11.3 %collective-permute-start.39 = (f32[2,8,34,1]{3,1,2,0:T(8,128)S(1)}, f32[2,8,34,1]{3,1,2,0:T(8,128)S(1)}, u32[]{:S(2)}, u32[]{:S(2)}) collective-permute-start(f32[2,8,34,1]{3,1,2,0:T(8,128)S(1)} %get-tuple-element.27), channel_id=1, source_target_pairs={{0,1},{1,2},{2,3},{3,0},{4,5},{5,6},{6,7},{7,4},{8,9},{9,10},{10,1... | collective-permute-start | bytes 6536 | tf_op jit(solution)/shard_map/ppermute | solution.py:22
where the time goes:
time: 255 us; the launch traced here: 251 us
  waiting for transfers between devices  112 us (44%)
  starting transfers between devices  63.1 us (25%)
  local copies, waits for them, and re-layouts  29.8 us (12%)
  blocking collectives  20.9 us (8%)
  matrix products  16.7 us (7%)
  other arithmetic  7.33 us (3%)
    ppermute x20, waiting for transfers between devices, with_halo(): lax.ppermute(tail, axis, [(i, (i + 1) % count) for i in range(count)])  52.5 us
    ppermute x20, waiting for transfers between devices, with_halo(): lax.ppermute(head, axis, [((i + 1) % count, i) for i in range(count)])  50.4 us
    ppermute x20, starting transfers between devices, with_halo(): lax.ppermute(tail, axis, [(i, (i + 1) % count) for i in range(count)])  32.3 us
    ppermute x20, starting transfers between devices, with_halo(): lax.ppermute(head, axis, [((i + 1) % count, i) for i in range(count)])  16 us
    gather x24, local copies, waits for them, and re-layouts  11 us
    all_to_all x1, blocking collectives, local(): lax.all_to_all(arranged, 'lat', split_axis=1, concat_axis=1, tiled=True)  8.3 us
    all_to_all x1, starting transfers between devices, local(): lax.all_to_all(gathered, 'lat', split_axis=1, concat_axis=1, tiled=True)  7.69 us
    dot_general x1, matrix products, spherical(): jnp.einsum('kcn,kirn->kicr', coefficients, legendre_blocks, preferred_ele...  7.06 us
  transfers between devices with their start and end apart: 43, of which 42 were waited for; matrix products, arithmetic and copies ran while one was open for 6% of the time, Pallas kernels for 0%

commit v1 on v0

--- a/solution.py
+++ b/solution.py
@@ -3,6 +3,8 @@
 import jax
 import jax.numpy as jnp
 from jax import lax
+from jax.experimental import pallas as pl
+from jax.experimental.pallas import tpu as pltpu
 from jax.sharding import PartitionSpec as P
 
 TIME_STEPS = 4
@@ -146,6 +148,497 @@
     return advance(height, east_flow, north_flow)
 
 
+EDGE = 8
+MESH = pl.DeviceIdType.MESH
+
+
+def turn(value, shift, axis):
+    size = value.shape[axis]
+    return pltpu.roll(value, shift % size, axis)
+
+
+def step_on_tile(height, east, north, keep, half, depth):
+    east_diff = turn(height, -1, 1) - turn(height, 1, 1)
+    north_diff = turn(height, -1, 0) - turn(height, 1, 0)
+    east = keep * east - half * east_diff
+    north = keep * north - half * north_diff
+    spread = (turn(east, -1, 1) - turn(east, 1, 1)) + (turn(north, -1, 0) - turn(north, 1, 0))
+    return height - depth * spread, east, north
+
+
+def unit_cosine(counts, period):
+    part = (counts & (period - 1)).astype(jnp.float32) * (1.0 / period)
+    angle = (jnp.abs(part - 0.5) - 0.25) * TWO_PI
+    square = angle * angle
+    series = -1.0 / 39916800.0
+    for denominator in (362880.0, -5040.0, 120.0, -6.0, 1.0):
+        series = series * square + 1.0 / denominator
+    return series * angle
+
+
+def split_pair(value):
+    high = value.astype(jnp.bfloat16)
+    return high, (value - high.astype(jnp.float32)).astype(jnp.bfloat16)
+
+
+def swap_chunks(parts, width):
+    count = len(parts)
+    lane = lax.broadcasted_iota(jnp.int32, parts[0].shape, 1) // width
+    parts = list(parts)
+    distance = 1
+    while distance < count:
+        upper = (lane // distance) % 2 == 1
+        for low in range(count):
+            if (low // distance) % 2 == 0:
+                first, second = parts[low], parts[low + distance]
+                parts[low] = jnp.where(upper, turn(second, width * distance, 1), first)
+                parts[low + distance] = jnp.where(upper, second, turn(first, -width * distance, 1))
+        distance *= 2
+    return parts
+
+
+def fused_kernel(
+    lat_count, lon_count, misfit, flow_east, flow_north, depth_in, drag_in, wet_in, table_in, love_in,
+    order_in, out_h, out_u, out_w, table, pack, rlon, rlat, rdepth, rdrag, rwet, coef, stepped, gath,
+    forward_table, inverse_table, order_col, weights, spec_out, spec_in, syn_out, syn, pack2, rlon2,
+    rw2, total, rh3, loading, table_sem, lat_send, lat_recv, lon_send, lon_recv, diag_send, diag_recv,
+    g_send, g_recv, a_send, a_recv, b_send, b_recv, c_send, c_recv, w_send, w_recv, p_send, p_recv,
+    h_send, h_recv,
+):
+    fields, rows, cols = misfit.shape
+    slots = table.shape[0]
+    used = table.shape[2]
+    period = cols * lon_count
+    ext_rows, ext_cols = rows + 2 * EDGE, 2 * cols
+    pair = 2 * slots
+    lat, lon = lax.axis_index("lat"), lax.axis_index("lon")
+    last = lat_count - 1
+    has_up, has_down = lat > 0, lat < last
+    left, right = lax.rem(lon + lon_count - 1, lon_count), lax.rem(lon + 1, lon_count)
+    table_copy = pltpu.make_async_copy(table_in.at[:, :, pl.ds(0, used)], table, table_sem)
+    table_copy.start()
+    barrier = pltpu.get_barrier_semaphore()
+
+    def hello(at_lat, at_lon):
+        pl.semaphore_signal(barrier, inc=1, device_id={"lat": at_lat, "lon": at_lon}, device_id_type=MESH)
+
+    @pl.when(lat == 0)
+    def _():
+        rlat[:, :, EDGE:, :] = jnp.zeros((3, fields, EDGE, cols), jnp.float32)
+        rdepth[EDGE:, :] = jnp.zeros((EDGE, cols), jnp.float32)
+        rdrag[EDGE:, :] = jnp.zeros((EDGE, cols), jnp.float32)
+        rwet[EDGE:, :] = jnp.zeros((EDGE, cols), jnp.int32)
+        rlon[:, :, rows + EDGE:, :] = jnp.zeros((2, 2, EDGE, cols), jnp.float32)
+        rw2[:, EDGE:, :] = jnp.zeros((fields, EDGE, cols), jnp.float32)
+        rh3[:, EDGE:, :] = jnp.zeros((fields, EDGE, cols), jnp.float32)
+
+    @pl.when(lat == last)
+    def _():
+        rlat[:, :, :EDGE, :] = jnp.zeros((3, fields, EDGE, cols), jnp.float32)
+        rdepth[:EDGE, :] = jnp.zeros((EDGE, cols), jnp.float32)
+        rdrag[:EDGE, :] = jnp.zeros((EDGE, cols), jnp.float32)
+        rwet[:EDGE, :] = jnp.zeros((EDGE, cols), jnp.int32)
+        rlon[:, :, rows:rows + EDGE, :] = jnp.zeros((2, 2, EDGE, cols), jnp.float32)
+        rw2[:, :EDGE, :] = jnp.zeros((fields, EDGE, cols), jnp.float32)
+        rh3[:, :EDGE, :] = jnp.zeros((fields, EDGE, cols), jnp.float32)
+
+    for d in range(1, lat_count):
+        hello(lax.rem(lat + d, lat_count), lon)
+    for d in range(1, lon_count):
+        hello(lat, lax.rem(lon + d, lon_count))
+
+    @pl.when(has_up)
+    def _():
+        hello(lat - 1, left)
+        hello(lat - 1, right)
+
+    @pl.when(has_down)
+    def _():
+        hello(lat + 1, left)
+        hello(lat + 1, right)
+
+    lane_own = lax.broadcasted_iota(jnp.int32, (rows, cols), 1)
+
+    def pack_edges(groups, target):
+        for t, group in enumerate(groups):
+            heads = jnp.zeros((rows, cols), jnp.float32)
+            tails = jnp.zeros((rows, cols), jnp.float32)
+            for s, value in enumerate(group):
+                here = lane_own // EDGE == s
+                heads = jnp.where(here, turn(value, EDGE * s, 1), heads)
+                tails = jnp.where(here, turn(value, EDGE * s + EDGE, 1), tails)
+            target[0, t] = heads
+            target[1, t] = tails
+
+    pack_edges(
+        (
+            [misfit[f] for f in range(fields)] + [flow_east[f] for f in range(fields)],
+            [flow_north[f] for f in range(fields)]
+            + [depth_in[...], drag_in[...], wet_in[...].astype(jnp.float32)],
+        ),
+        pack,
+    )
+    sides = has_up.astype(jnp.int32) + has_down.astype(jnp.int32)
+    pl.semaphore_wait(barrier, lat_count + lon_count - 2 + 2 * sides)
+
+    def remote(source, target, send, recv, at_lat, at_lon):
+        return pltpu.make_async_remote_copy(
+            src_ref=source, dst_ref=target, send_sem=send, recv_sem=recv,
+            device_id={"lat": at_lat, "lon": at_lon}, device_id_type=MESH,
+        )
+
+    def lat_copies(up):
+        here = pl.ds(0, EDGE) if up else pl.ds(rows - EDGE, EDGE)
+        there = pl.ds(0, EDGE) if up else pl.ds(EDGE, EDGE)
+        at = lat - 1 if up else lat + 1
+        k = 0 if up else 1
+        pairs = [
+            (misfit.at[:, here], rlat.at[0, :, there]),
+            (flow_east.at[:, here], rlat.at[1, :, there]),
+            (flow_north.at[:, here], rlat.at[2, :, there]),
+            (depth_in.at[here], rdepth.at[there]),
+            (drag_in.at[here], rdrag.at[there]),
+            (wet_in.at[here], rwet.at[there]),
+        ]
+        copies = [
+            remote(s, t, lat_send.at[k, n], lat_recv.at[k, n], at, lon) for n, (s, t) in enumerate(pairs)
+        ]
+        corner = pl.ds(rows, EDGE) if up else pl.ds(rows + EDGE, EDGE)
+        for side, at_lon in ((0, left), (1, right)):
+            n = 2 * k + side
+            copies.append(
+                remote(
+                    pack.at[side, :, here], rlon.at[side, :, corner], diag_send.at[n], diag_recv.at[n], at, at_lon
+                )
+            )
+        return copies
+
+    lon_copies = [
+        remote(pack.at[s], rlon.at[s, :, pl.ds(0, rows)], lon_send.at[s], lon_recv.at[s], lat, at)
+        for s, at in ((0, left), (1, right))
+    ]
+
+    def on_sides(make, act_up, act_down):
+        @pl.when(has_up)
+        def _():
+            for copy in make(True):
+                act_up(copy)
+
+        @pl.when(has_down)
+        def _():
+            for copy in make(False):
+                act_down(copy)
+
+    def start(copy):
+        copy.start()
+
+    def wait_send(copy):
+        copy.wait_send()
+
+    def wait_recv_sides(make):
+        @pl.when(has_down)
+        def _():
+            for copy in make(True):
+                copy.wait_recv()
+
+        @pl.when(has_up)
+        def _():
+            for copy in make(False):
+                copy.wait_recv()
+
+    on_sides(lat_copies, start, start)
+    for copy in lon_copies:
+        copy.start()
+
+    orders = period // 2
+    span = 2 * orders
+    row_id = lax.broadcasted_iota(jnp.int32, (span, orders), 0) // 2
+    position_id = lax.broadcasted_iota(jnp.int32, (span, orders), 1)
+    chosen = jnp.where(row_id == position_id, order_in[...].astype(jnp.float32), 0.0)
+    order_col[...] = jnp.sum(chosen, axis=1, keepdims=True).astype(jnp.int32)
+
+    block = lat_count * pair
+    parity = (lax.broadcasted_iota(jnp.int32, (block, ext_cols), 0) % 2) * (period // 4)
+    lane_ext = lax.broadcasted_iota(jnp.int32, (block, ext_cols), 1)
+    shifted = jnp.where(lane_ext < cols + cols // 2, lane_ext, lane_ext - ext_cols) + lon * cols
+    for j in range(lon_count):
+        order_here = order_col[pl.ds(j * block, block), :]
+        value = unit_cosine(order_here * shifted + parity, period)
+        value = value * jnp.where(order_here == 0, 1.0, 2.0)
+        inverse_table[0, j], inverse_table[1, j] = split_pair(value)
+    mine = order_col[pl.ds(pl.multiple_of(lon * block, block), block), :]
+    lane_full = lax.broadcasted_iota(jnp.int32, (block, cols), 1)
+    for j in range(lon_count):
+        value = unit_cosine(mine * (lane_full + j * cols) + parity[:, :cols], period)
+        forward_table[j, 0:block], forward_table[j, block:] = split_pair(value)
+
+    degree_row = lax.broadcasted_iota(jnp.int32, (orders, used), 0)
+    degree_lane = lax.broadcasted_iota(jnp.int32, (orders, used), 1)
+    diagonal = lax.broadcasted_iota(jnp.int32, (orders, orders), 0) == lax.broadcasted_iota(
+        jnp.int32, (orders, orders), 1
+    )
+    love_col = jnp.sum(jnp.where(diagonal, love_in[...], 0.0), axis=1, keepdims=True)
+    offset = degree_row - degree_lane
+    first = (lon * lat_count + lat) * slots
+    for p in range(slots):
+        order_here = order_col[pl.ds(2 * (first + p), 1), :]
+        weights[p:p + 1, :] = jnp.sum(jnp.where(offset == order_here, love_col, 0.0), axis=0, keepdims=True)
+
+    wait_recv_sides(lat_copies)
+    for copy in lon_copies:
+        copy.wait_recv()
+
+    lane_tall = lax.broadcasted_iota(jnp.int32, (ext_rows, cols), 1)
+
+    def assemble(own, beside, ahead, behind, slot):
+        main = jnp.concatenate([own, beside], axis=0)
+        ahead = turn_to(ahead, cols - EDGE * slot)
+        behind = turn_to(behind, 2 * cols - EDGE - EDGE * slot)
+        extra = jnp.where(lane_tall < EDGE, ahead, jnp.where(lane_tall >= cols - EDGE, behind, 0.0))
+        return jnp.concatenate([main, extra], axis=1)
+
+    def turn_to(value, shift):
+        return pltpu.roll(value, shift % cols if isinstance(shift, int) else lax.rem(shift, cols), 1)
+
+    depth_ext = assemble(depth_in[...], rdepth[...], rlon[0, 1], rlon[1, 1], fields)
+    drag_ext = assemble(drag_in[...], rdrag[...], rlon[0, 1], rlon[1, 1], fields + 1)
+    wet_ext = assemble(
+        wet_in[...].astype(jnp.float32), rwet[...].astype(jnp.float32), rlon[0, 1], rlon[1, 1], fields + 2
+    )
+    coef[0] = wet_ext * (1.0 - drag_ext)
+    coef[1] = 0.5 * wet_ext
+    coef[2] = 0.5 * wet_ext * depth_ext
+    coef[3] = wet_ext
+
+    @pl.loop(0, fields)
+    def _(f):
+        keep, half, depth, wet = coef[0], coef[1], coef[2], coef[3]
+        height = wet * assemble(misfit[f], rlat[0, f], rlon[0, 0], rlon[1, 0], f)
+        east = wet * assemble(flow_east[f], rlat[1, f], rlon[0, 0], rlon[1, 0], f + fields)
+        north = wet * assemble(flow_north[f], rlat[2, f], rlon[0, 1], rlon[1, 1], f)
+        for _ in range(TIME_STEPS):
+            height, east, north = step_on_tile(height, east, north, keep, half, depth)
+        height = height[:rows, :cols]
+        stepped[0, f] = height
+        stepped[1, f] = east[:rows, :cols]
+        stepped[2, f] = north[:rows, :cols]
+        gath[lon, pl.ds(pl.multiple_of(f * rows, rows), rows), :] = height.astype(jnp.bfloat16)
+
+    def lon_gather(ref, send, recv):
+        return [
+            remote(ref.at[lon], ref.at[lon], send.at[d - 1], recv.at[d - 1], lat, lax.rem(lon + d, lon_count))
+            for d in range(1, lon_count)
+        ]
+
+    def source(d):
+        return lax.rem(lon + lon_count - d, lon_count)
+
+    g_copies = lon_gather(gath, g_send, g_recv)
+    for copy in g_copies:
+        copy.start()
+
+    pack_edges(([stepped[k, f] for k in range(2) for f in range(fields)],), pack2)
+
+    def w_copies(up):
+        here = pl.ds(0, EDGE) if up else pl.ds(rows - EDGE, EDGE)
+        there = pl.ds(0, EDGE) if up else pl.ds(EDGE, EDGE)
+        k = 0 if up else 1
+        at = lat - 1 if up else lat + 1
+        return [remote(stepped.at[2, :, here], rw2.at[:, there], w_send.at[k], w_recv.at[k], at, lon)]
+
+    p_copies = [
+        remote(pack2.at[s, 0], rlon2.at[s, pl.ds(0, rows)], p_send.at[s], p_recv.at[s], lat, at)
+        for s, at in ((0, left), (1, right))
+    ]
+
+    def transform(j):
+        return lax.dot_general(
+            forward_table[j], gath[j], (((1,), (1,)), ((), ())), preferred_element_type=jnp.float32
+        )
+
+    both = transform(lon)
+    for d in range(1, lon_count):
+        g_copies[d - 1].wait_recv()
+        both = both + transform(source(d))
+    spectra = (both[:block] + both[block:]).astype(jnp.bfloat16)
+    for i in range(lat_count):
+        spec_out[i] = spectra[i * pair:(i + 1) * pair]
+
+    def lat_exchange(ref, target, slot, send, recv):
+        copies = []
+        for d in range(1, lat_count):
+            peer = lax.rem(lat + d, lat_count)
+            copies.append(remote(ref.at[peer], slot, send.at[d - 1], recv.at[d - 1], peer, lon))
+        return copies
+
+    a_copies = lat_exchange(spec_out, spec_in, spec_in.at[lat], a_send, a_recv)
+    for copy in a_copies:
+        copy.start()
+    on_sides(w_copies, start, start)
+    for copy in p_copies:
+        copy.start()
+    spec_in[lat] = spec_out[lat]
+    table_copy.wait()
+    for copy in a_copies:
+        copy.wait_recv()
+    by_field = swap_chunks([spec_in[i].astype(jnp.float32) for i in range(lat_count)], rows)
+    arranged = jnp.concatenate(by_field, axis=0).astype(jnp.bfloat16)
+    slot_of_row = (lax.broadcasted_iota(jnp.int32, (fields * pair, used), 0) // 2) % slots
+    coefficients = jnp.zeros((fields * pair, used), jnp.float32)
+    for p in range(slots):
+        product = jnp.dot(arranged, table[p], preferred_element_type=jnp.float32)
+        coefficients = jnp.where(slot_of_row == p, product * weights[p:p + 1, :], coefficients)
+    synthesis = jnp.zeros((fields * pair, table.shape[1]), jnp.float32)
+    for p in range(slots):
+        synthesis = synthesis + lax.dot_general(
+            jnp.where(slot_of_row == p, coefficients, 0.0).astype(jnp.bfloat16),
+            table[p],
+            (((1,), (1,)), ((), ())),
+            preferred_element_type=jnp.float32,
+        )
+    by_lat = swap_chunks([synthesis[f * pair:(f + 1) * pair] for f in range(fields)], rows)
+    for i in range(lat_count):
+        syn_out[i] = by_lat[i].astype(jnp.bfloat16)
+    b_copies = lat_exchange(syn_out, syn, syn.at[lon, lat], b_send, b_recv)
+    for copy in b_copies:
+        copy.start()
+    syn[lon, lat] = syn_out[lat]
+    for copy in b_copies:
+        copy.wait_recv()
+    c_copies = lon_gather(syn, c_send, c_recv)
+    for copy in c_copies:
+        copy.start()
+
+    def back(j):
+        stacked = syn[j].reshape(block, fields * rows)
+        contract = (((0,), (0,)), ((), ()))
+        return lax.dot_general(
+            stacked, inverse_table[0, j], contract, preferred_element_type=jnp.float32
+        ) + lax.dot_general(stacked, inverse_table[1, j], contract, preferred_element_type=jnp.float32)
+
+    load = back(lon)
+    for d in range(1, lon_count):
+        c_copies[d - 1].wait_recv()
+        load = load + back(source(d))
+    wet_own = wet_in[...].astype(jnp.float32)
+    for f in range(fields):
+        part = load[f * rows:(f + 1) * rows]
+        total[f] = stepped[0, f] + wet_own * part[:, :cols]
+        loading[f] = part[:, cols:]
+
+    def h_copies(up):
+        here = pl.ds(0, EDGE) if up else pl.ds(rows - EDGE, EDGE)
+        there = pl.ds(0, EDGE) if up else pl.ds(EDGE, EDGE)
+        k = 0 if up else 1
+        at = lat - 1 if up else lat + 1
+        return [remote(total.at[:, here], rh3.at[:, there], h_send.at[k], h_recv.at[k], at, lon)]
+
+    on_sides(h_copies, start, start)
+    for copy in p_copies:
+        copy.wait_recv()
+    wait_recv_sides(w_copies)
+    wait_recv_sides(h_copies)
+    rlon2[:, rows:, :] = jnp.zeros((2, 2 * EDGE, cols), jnp.float32)
+
+    @pl.loop(0, fields)
+    def _(f):
+        keep, half, depth, wet = coef[0], coef[1], coef[2], coef[3]
+        height = assemble(total[f], rh3[f], rlon2[0], rlon2[1], f)
+        none = jnp.zeros((2 * EDGE, cols), jnp.float32)
+        beyond = jnp.concatenate([loading[f], none], axis=0)
+        beyond = jnp.concatenate([jnp.zeros((ext_rows, cols), jnp.float32), beyond], axis=1)
+        height = height + wet * beyond
+        east = assemble(stepped[1, f], none, rlon2[0], rlon2[1], f + fields)
+        north = assemble(stepped[2, f], rw2[f], jnp.zeros((ext_rows, cols), jnp.float32), jnp.zeros((ext_rows, cols), jnp.float32), 0)
+        height, east, north = step_on_tile(height, east, north, keep, half, depth)
+        out_h[f] = height[:rows, :cols]
+        out_u[f] = east[:rows, :cols]
+        out_w[f] = north[:rows, :cols]
+
+    on_sides(lat_copies, wait_send, wait_send)
+    on_sides(w_copies, wait_send, wait_send)
+    on_sides(h_copies, wait_send, wait_send)
+    for copy in lon_copies + g_copies + p_copies + a_copies + b_copies + c_copies:
+        copy.wait_send()
+
+
+def fused(misfit, flow_east, flow_north, ocean_depth, drag_rate, wet_mask, legendre, love_factor, assignment):
+    fields, rows, cols = misfit.shape
+    lat_count = lax.axis_size("lat")
+    lon_count = lax.axis_size("lon")
+    slots, lats, degrees = legendre.shape
+    orders = lon_count * cols // 2
+    used = min(degrees, orders)
+    pair = 2 * slots
+    block = lat_count * pair
+    f32, b16 = jnp.float32, jnp.bfloat16
+    ext_rows = rows + 2 * EDGE
+    tile = jax.ShapeDtypeStruct((fields, rows, cols), f32)
+    vmem = pl.BlockSpec(memory_space=pltpu.VMEM)
+    dma = pltpu.SemaphoreType.DMA
+    return pl.pallas_call(
+        lambda *refs: fused_kernel(lat_count, lon_count, *refs),
+        out_shape=(tile, tile, tile),
+        in_specs=[vmem] * 6 + [pl.BlockSpec(memory_space=pl.ANY)] + [vmem] * 2,
+        out_specs=(vmem, vmem, vmem),
+        scratch_shapes=[
+            pltpu.VMEM((slots, lats, used), b16),
+            pltpu.VMEM((2, 2, rows, cols), f32),
+            pltpu.VMEM((2, 2, ext_rows, cols), f32),
+            pltpu.VMEM((3, fields, 2 * EDGE, cols), f32),
+            pltpu.VMEM((2 * EDGE, cols), f32),
+            pltpu.VMEM((2 * EDGE, cols), f32),
+            pltpu.VMEM((2 * EDGE, cols), jnp.int32),
+            pltpu.VMEM((4, ext_rows, 2 * cols), f32),
+            pltpu.VMEM((3, fields, rows, cols), f32),
+            pltpu.VMEM((lon_count, fields * rows, cols), b16),
+            pltpu.VMEM((lon_count, 2 * block, cols), b16),
+            pltpu.VMEM((2, lon_count, block, 2 * cols), b16),
+            pltpu.VMEM((2 * orders, 1), jnp.int32),
+            pltpu.VMEM((slots, used), f32),
+            pltpu.VMEM((lat_count, pair, fields * rows), b16),
+            pltpu.VMEM((lat_count, pair, fields * rows), b16),
+            pltpu.VMEM((lat_count, pair, fields * rows), b16),
+            pltpu.VMEM((lon_count, lat_count, pair, fields * rows), b16),
+            pltpu.VMEM((2, 1, rows, cols), f32),
+            pltpu.VMEM((2, ext_rows, cols), f32),
+            pltpu.VMEM((fields, 2 * EDGE, cols), f32),
+            pltpu.VMEM((fields, rows, cols), f32),
+            pltpu.VMEM((fields, 2 * EDGE, cols), f32),
+            pltpu.VMEM((fields, rows, cols), f32),
+            dma,
+            dma((2, 6)), dma((2, 6)), dma((2,)), dma((2,)), dma((4,)), dma((4,)),
+            dma((lon_count - 1,)), dma((lon_count - 1,)),
+            dma((lat_count - 1,)), dma((lat_count - 1,)), dma((lat_count - 1,)), dma((lat_count - 1,)),
+            dma((lon_count - 1,)), dma((lon_count - 1,)),
+            dma((2,)), dma((2,)), dma((2,)), dma((2,)), dma((2,)), dma((2,)),
+        ],
+        compiler_params=pltpu.CompilerParams(
+            collective_id=0, has_side_effects=True, vmem_limit_bytes=40 * 1024 * 1024
+        ),
+    )(
+        misfit, flow_east, flow_north, ocean_depth, drag_rate, wet_mask, legendre,
+        love_factor.reshape(1, -1), assignment.reshape(1, -1),
+    )
+
+
+def whole(*arrays):
+    misfit, legendre = arrays[0], arrays[6]
+    fields, rows, cols = misfit.shape
+    lat_count = lax.axis_size("lat")
+    lon_count = lax.axis_size("lon")
+    fits = (
+        fields == lat_count
+        and legendre.shape[0] % 8 == 0
+        and cols == 16 * EDGE
+        and fields * EDGE * 2 <= cols
+        and rows % 32 == 0
+        and lon_count > 2
+        and (cols * lon_count) & (cols * lon_count - 1) == 0
+    )
+    return fused(*arrays) if fits else local(*arrays)
+
+
 def solution(mesh):
     placed = (
         P(None, "lat", "lon"),
@@ -159,7 +652,7 @@
         P(),
     )
     return jax.shard_map(
-        local,
+        whole,
         mesh=mesh,
         in_specs=placed,
         out_specs=(P(None, "lat", "lon"), P(None, "lat", "lon"), P(None, "lat", "lon")),

time: 255 us -> 52 us (0.20); the launches traced: 251 us -> 51.5 us
  waiting for transfers between devices: 112 us -> 0 us
  starting transfers between devices: 63.1 us -> 0 us
  Pallas kernels: 0 us -> 40.5 us
  blocking collectives: 20.9 us -> 0 us
  local copies, waits for them, and re-layouts: 29.8 us -> 10.4 us
  matrix products: 16.7 us -> 0 us
  other arithmetic: 7.33 us -> 0 us
    ppermute x40 -> x0, waiting for transfers between devices: 103 us -> none  [the longest x20 52.5 us: with_halo(): lax.ppermute(tail, axis, [(i, (i + 1) % count) for i in range(count)])]
    ppermute x40 -> x0, starting transfers between devices: 48.3 us -> none  [the longest x20 32.3 us: with_halo(): lax.ppermute(tail, axis, [(i, (i + 1) % count) for i in range(count)])]
    pallas_call x0 -> x1, Pallas kernels: none -> 40.5 us  [fused(): pl.pallas_call(lambda *refs: fused_kernel(lat_count, lon_count, *refs), o...]
    all_to_all x3 -> x0, blocking collectives: 20.9 us -> none  [the longest x1 8.3 us: local(): lax.all_to_all(arranged, 'lat', split_axis=1, concat_axis=1, tiled=True)]
    dot_general x5 -> x0, matrix products: 16.7 us -> none  [the longest x1 7.06 us: spherical(): jnp.einsum('kcn,kirn->kicr', coefficients, legendre_blocks, preferred_ele...]
    all_to_all x3 -> x0, starting transfers between devices: 14.8 us -> none  [the longest x1 7.69 us: local(): lax.all_to_all(gathered, 'lat', split_axis=1, concat_axis=1, tiled=True)]
    gather x24 -> x0, local copies, waits for them, and re-layouts: 11 us -> none
    all_to_all x3 -> x0, waiting for transfers between devices: 8.78 us -> none  [the longest x1 5.09 us: local(): lax.all_to_all(gathered, 'lat', split_axis=1, concat_axis=1, tiled=True)]
  transfers between devices with their start and end apart: 43 -> 0, of which waited for: 42 -> 0; matrix products, arithmetic and copies ran while one was open for 6% -> 0% of each run, Pallas kernels for 0% -> 0%
where the time goes in v1:
time: 52 us; the launch traced here: 51.5 us
  Pallas kernels  40.5 us (78%)
  local copies, waits for them, and re-layouts  10.4 us (20%)
  between operations  0.66 us (1%)
    pallas_call x1, Pallas kernels, fused(): pl.pallas_call(lambda *refs: fused_kernel(lat_count, lon_count, *refs), o...  40.5 us
    unnamed x21, local copies, waits for them, and re-layouts  10.4 us

profile of v1, /device:TPU:1, one launch (start us, length us, event | category | flops | bytes accessed | tf_op | source)
XLA Modules:
  0.0 51.5 jit_solution(8184151413365721847)
XLA Ops:
  0.6 0.0 copy-start
  0.6 2.2 %copy-done = bf16[8,256,1024]{2,1,0:T(8,128)(2,1)S(1)} copy-done((bf16[8,256,1024]{2,1,0:T(8,128)(2,1)S(1)}, bf16[8,256,1024]{2,1,0:T(8,128)(2,1)}, u32[]{:S(2)}) %copy-start) | copy-done | bytes 4194328
  2.8 0.0 copy-start.1
  2.8 0.9 %copy-done.1 = f32[8,32,128]{2,1,0:T(8,128)S(1)} copy-done((f32[8,32,128]{2,1,0:T(8,128)S(1)}, f32[8,32,128]{2,1,0:T(8,128)}, u32[]{:S(2)}) %copy-start.1) | copy-done | bytes 131096
  3.7 0.0 copy-start.2
  3.7 0.9 %copy-done.2 = f32[8,32,128]{2,1,0:T(8,128)S(1)} copy-done((f32[8,32,128]{2,1,0:T(8,128)S(1)}, f32[8,32,128]{2,1,0:T(8,128)}, u32[]{:S(2)}) %copy-start.2) | copy-done | bytes 131096
  4.6 0.0 copy-start.3
  4.6 0.9 %copy-done.3 = f32[8,32,128]{2,1,0:T(8,128)S(1)} copy-done((f32[8,32,128]{2,1,0:T(8,128)S(1)}, f32[8,32,128]{2,1,0:T(8,128)}, u32[]{:S(2)}) %copy-start.3) | copy-done | bytes 131096
  5.5 0.0 copy-start.4
  5.5 0.7 %copy-done.4 = f32[32,128]{1,0:T(8,128)S(1)} copy-done((f32[32,128]{1,0:T(8,128)S(1)}, f32[32,128]{1,0:T(8,128)}, u32[]{:S(2)}) %copy-start.4) | copy-done | bytes 16408
  6.3 0.0 copy-start.5
  6.3 0.7 %copy-done.5 = f32[32,128]{1,0:T(8,128)S(1)} copy-done((f32[32,128]{1,0:T(8,128)S(1)}, f32[32,128]{1,0:T(8,128)}, u32[]{:S(2)}) %copy-start.5) | copy-done | bytes 16408
  7.0 0.0 copy-start.6
  7.0 0.7 %copy-done.6 = s32[32,128]{1,0:T(8,128)S(1)} copy-done((s32[32,128]{1,0:T(8,128)S(1)}, s32[32,128]{1,0:T(8,128)}, u32[]{:S(2)}) %copy-start.6) | copy-done | bytes 16408
  7.7 0.0 copy-start.7
  7.7 0.7 %copy-done.7 = f32[256]{0:T(256)S(1)} copy-done((f32[256]{0:T(256)S(1)}, f32[256]{0:T(256)}, u32[]{:S(2)}) %copy-start.7) | copy-done | bytes 1048
  8.4 0.0 copy-start.8
  8.4 0.7 %copy-done.8 = s32[256]{0:T(256)S(1)} copy-done((s32[256]{0:T(256)S(1)}, s32[256]{0:T(256)}, u32[]{:S(2)}) %copy-start.8) | copy-done | bytes 1048
  9.0 40.5 %shard_map.112 = (f32[8,32,128]{2,1,0:T(8,128)S(1)}, f32[8,32,128]{2,1,0:T(8,128)S(1)}, f32[8,32,128]{2,1,0:T(8,128)S(1)}) custom-call(f32[8,32,128]{2,1,0:T(8,128)S(1)} %copy-done.1, f32[8,32,128]{2,1,0:T(8,128)S(1)} %copy-done.2, f32[8,32,128]{2,1,0:T(8,128)S(1)} %copy-done.3, f32[32,128]{1,0:T(8,128)S(1)} %copy-done.4, f32[32,128]{1,0:T(8,128)S(1)} %copy-done.5, ...), custom_call_target="tpu_custom_call" | custom-call | tf_op jit(solution)/shard_map/pallas_call | solution.py:579
  49.5 0.7 %copy.15 = f32[8,32,128]{2,1,0:T(8,128)} copy(f32[8,32,128]{2,1,0:T(8,128)S(1)} %get-tuple-element.6) | data formatting | bytes 262144
  50.2 0.7 %copy.16 = f32[8,32,128]{2,1,0:T(8,128)} copy(f32[8,32,128]{2,1,0:T(8,128)S(1)} %get-tuple-element.7) | data formatting | bytes 262144
  50.8 0.7 %copy.17 = f32[8,32,128]{2,1,0:T(8,128)} copy(f32[8,32,128]{2,1,0:T(8,128)S(1)} %get-tuple-element.8) | data formatting | bytes 262144
Async XLA Ops:
  0.6 2.2 %copy-start = (bf16[8,256,1024]{2,1,0:T(8,128)(2,1)S(1)}, bf16[8,256,1024]{2,1,0:T(8,128)(2,1)}, u32[]{:S(2)}) copy-start(bf16[8,256,1024]{2,1,0:T(8,128)(2,1)} %refs_6_.1) | copy-start | bytes 12582916
  2.8 0.9 %copy-start.1 = (f32[8,32,128]{2,1,0:T(8,128)S(1)}, f32[8,32,128]{2,1,0:T(8,128)}, u32[]{:S(2)}) copy-start(f32[8,32,128]{2,1,0:T(8,128)} %refs_0_.1) | copy-start | bytes 393220
  3.7 0.9 %copy-start.2 = (f32[8,32,128]{2,1,0:T(8,128)S(1)}, f32[8,32,128]{2,1,0:T(8,128)}, u32[]{:S(2)}) copy-start(f32[8,32,128]{2,1,0:T(8,128)} %refs_1_.1) | copy-start | bytes 393220
  4.6 0.9 %copy-start.3 = (f32[8,32,128]{2,1,0:T(8,128)S(1)}, f32[8,32,128]{2,1,0:T(8,128)}, u32[]{:S(2)}) copy-start(f32[8,32,128]{2,1,0:T(8,128)} %refs_2_.1) | copy-start | bytes 393220
  5.5 0.7 %copy-start.4 = (f32[32,128]{1,0:T(8,128)S(1)}, f32[32,128]{1,0:T(8,128)}, u32[]{:S(2)}) copy-start(f32[32,128]{1,0:T(8,128)} %refs_3_.1) | copy-start | bytes 49156
  6.3 0.7 %copy-start.5 = (f32[32,128]{1,0:T(8,128)S(1)}, f32[32,128]{1,0:T(8,128)}, u32[]{:S(2)}) copy-start(f32[32,128]{1,0:T(8,128)} %refs_4_.1) | copy-start | bytes 49156
  7.0 0.7 %copy-start.6 = (s32[32,128]{1,0:T(8,128)S(1)}, s32[32,128]{1,0:T(8,128)}, u32[]{:S(2)}) copy-start(s32[32,128]{1,0:T(8,128)} %refs_5_.1) | copy-start | bytes 49156
  7.7 0.7 %copy-start.7 = (f32[256]{0:T(256)S(1)}, f32[256]{0:T(256)}, u32[]{:S(2)}) copy-start(f32[256]{0:T(256)} %param.16) | copy-start | bytes 3076
  8.4 0.7 %copy-start.8 = (s32[256]{0:T(256)S(1)}, s32[256]{0:T(256)}, u32[]{:S(2)}) copy-start(s32[256]{0:T(256)} %param.17) | copy-start | bytes 3076

commit v2 on v1

--- a/solution.py
+++ b/solution.py
@@ -198,14 +198,15 @@
 
 
 def fused_kernel(
-    lat_count, lon_count, misfit, flow_east, flow_north, depth_in, drag_in, wet_in, table_in, love_in,
-    order_in, out_h, out_u, out_w, table, pack, rlon, rlat, rdepth, rdrag, rwet, coef, stepped, gath,
+    lat_count, lon_count, misfit_far, east_far, north_far, depth_far, drag_far, wet_far, table_in, love_far,
+    order_far, out_h, out_u, out_w, table, pack, rlon, rlat, rdepth, rdrag, rwet, coef, stepped, gath,
     forward_table, inverse_table, order_col, weights, spec_out, spec_in, syn_out, syn, pack2, rlon2,
-    rw2, total, rh3, loading, table_sem, lat_send, lat_recv, lon_send, lon_recv, diag_send, diag_recv,
+    rw2, total, rh3, loading, own, depth_in, drag_in, wet_in, love_in, order_in, own_sem, table_sem, lat_send, lat_recv, lon_send, lon_recv, diag_send, diag_recv,
     g_send, g_recv, a_send, a_recv, b_send, b_recv, c_send, c_recv, w_send, w_recv, p_send, p_recv,
     h_send, h_recv,
 ):
-    fields, rows, cols = misfit.shape
+    misfit, flow_east, flow_north = own.at[0], own.at[1], own.at[2]
+    fields, rows, cols = misfit_far.shape
     slots = table.shape[0]
     used = table.shape[2]
     period = cols * lon_count
@@ -215,8 +216,18 @@
     last = lat_count - 1
     has_up, has_down = lat > 0, lat < last
     left, right = lax.rem(lon + lon_count - 1, lon_count), lax.rem(lon + 1, lon_count)
+    own_copies = [
+        pltpu.make_async_copy(far, near, own_sem.at[n])
+        for n, (far, near) in enumerate(
+            [
+                (misfit_far, misfit), (east_far, flow_east), (north_far, flow_north), (depth_far, depth_in),
+                (drag_far, drag_in), (wet_far, wet_in), (love_far, love_in), (order_far, order_in),
+            ]
+        )
+    ]
+    for copy in own_copies:
+        copy.start()
     table_copy = pltpu.make_async_copy(table_in.at[:, :, pl.ds(0, used)], table, table_sem)
-    table_copy.start()
     barrier = pltpu.get_barrier_semaphore()
 
     def hello(at_lat, at_lon):
@@ -270,6 +281,9 @@
             target[0, t] = heads
             target[1, t] = tails
 
+    for copy in own_copies:
+        copy.wait()
+    table_copy.start()
     pack_edges(
         (
             [misfit[f] for f in range(fields)] + [flow_east[f] for f in range(fields)],
@@ -293,12 +307,12 @@
         at = lat - 1 if up else lat + 1
         k = 0 if up else 1
         pairs = [
-            (misfit.at[:, here], rlat.at[0, :, there]),
-            (flow_east.at[:, here], rlat.at[1, :, there]),
-            (flow_north.at[:, here], rlat.at[2, :, there]),
-            (depth_in.at[here], rdepth.at[there]),
-            (drag_in.at[here], rdrag.at[there]),
-            (wet_in.at[here], rwet.at[there]),
+            (misfit_far.at[:, here], rlat.at[0, :, there]),
+            (east_far.at[:, here], rlat.at[1, :, there]),
+            (north_far.at[:, here], rlat.at[2, :, there]),
+            (depth_far.at[here], rdepth.at[there]),
+            (drag_far.at[here], rdrag.at[there]),
+            (wet_far.at[here], rwet.at[there]),
         ]
         copies = [
             remote(s, t, lat_send.at[k, n], lat_recv.at[k, n], at, lon) for n, (s, t) in enumerate(pairs)
@@ -503,11 +517,18 @@
     for copy in b_copies:
         copy.start()
     syn[lon, lat] = syn_out[lat]
-    for copy in b_copies:
-        copy.wait_recv()
-    c_copies = lon_gather(syn, c_send, c_recv)
-    for copy in c_copies:
-        copy.start()
+    c_copies = []
+    for e in range(lat_count):
+        from_lat = lax.rem(lat + lat_count - e, lat_count)
+        if e:
+            b_copies[e - 1].wait_recv()
+        for d in range(1, lon_count):
+            copy = remote(
+                syn.at[lon, from_lat], syn.at[lon, from_lat], c_send.at[d - 1, e], c_recv.at[d - 1, e],
+                lat, lax.rem(lon + d, lon_count),
+            )
+            copy.start()
+            c_copies.append(copy)
 
     def back(j):
         stacked = syn[j].reshape(block, fields * rows)
@@ -518,7 +539,8 @@
 
     load = back(lon)
     for d in range(1, lon_count):
-        c_copies[d - 1].wait_recv()
+        for e in range(lat_count):
+            c_copies[e * (lon_count - 1) + d - 1].wait_recv()
         load = load + back(source(d))
     wet_own = wet_in[...].astype(jnp.float32)
     for f in range(fields):
@@ -579,7 +601,7 @@
     return pl.pallas_call(
         lambda *refs: fused_kernel(lat_count, lon_count, *refs),
         out_shape=(tile, tile, tile),
-        in_specs=[vmem] * 6 + [pl.BlockSpec(memory_space=pl.ANY)] + [vmem] * 2,
+        in_specs=[pl.BlockSpec(memory_space=pltpu.HBM)] * 9,
         out_specs=(vmem, vmem, vmem),
         scratch_shapes=[
             pltpu.VMEM((slots, lats, used), b16),
@@ -606,15 +628,22 @@
             pltpu.VMEM((fields, rows, cols), f32),
             pltpu.VMEM((fields, 2 * EDGE, cols), f32),
             pltpu.VMEM((fields, rows, cols), f32),
+            pltpu.VMEM((3, fields, rows, cols), f32),
+            pltpu.VMEM((rows, cols), f32),
+            pltpu.VMEM((rows, cols), f32),
+            pltpu.VMEM((rows, cols), jnp.int32),
+            pltpu.VMEM((1, orders), f32),
+            pltpu.VMEM((1, orders), jnp.int32),
+            dma((8,)),
             dma,
             dma((2, 6)), dma((2, 6)), dma((2,)), dma((2,)), dma((4,)), dma((4,)),
             dma((lon_count - 1,)), dma((lon_count - 1,)),
             dma((lat_count - 1,)), dma((lat_count - 1,)), dma((lat_count - 1,)), dma((lat_count - 1,)),
-            dma((lon_count - 1,)), dma((lon_count - 1,)),
+            dma((lon_count - 1, lat_count)), dma((lon_count - 1, lat_count)),
             dma((2,)), dma((2,)), dma((2,)), dma((2,)), dma((2,)), dma((2,)),
         ],
         compiler_params=pltpu.CompilerParams(
-            collective_id=0, has_side_effects=True, vmem_limit_bytes=40 * 1024 * 1024
+            collective_id=0, has_side_effects=True, vmem_limit_bytes=67043328
         ),
     )(
         misfit, flow_east, flow_north, ocean_depth, drag_rate, wet_mask, legendre,

time: 52 us -> 46.7 us (0.90)
  local copies, waits for them, and re-layouts: 10.4 us -> 4.7 us
  Pallas kernels: 40.5 us -> 41.2 us
    unnamed x21 -> x3, local copies, waits for them, and re-layouts: 10.4 us -> 4.7 us
    pallas_call x1, Pallas kernels: 40.5 us -> 41.2 us  [fused(): pl.pallas_call(lambda *refs: fused_kernel(lat_count, lon_count, *refs), o...]
where the time goes in v2:
time: 46.7 us; the launch traced here: 46.5 us
  Pallas kernels  41.2 us (88%)
  local copies, waits for them, and re-layouts  4.7 us (10%)
  between operations  0.64 us (1%)
    pallas_call x1, Pallas kernels, fused(): pl.pallas_call(lambda *refs: fused_kernel(lat_count, lon_count, *refs), o...  41.2 us
    unnamed x3, local copies, waits for them, and re-layouts  4.7 us

profile of v2, /device:TPU:1, one launch (start us, length us, event | category | flops | bytes accessed | tf_op | source)
XLA Modules:
  0.0 46.5 jit_solution(3326517273743020526)
XLA Ops:
  0.6 41.2 %shard_map.112 = (f32[8,32,128]{2,1,0:T(8,128)}, f32[8,32,128]{2,1,0:T(8,128)}, f32[8,32,128]{2,1,0:T(8,128)}) custom-call(f32[8,32,128]{2,1,0:T(8,128)} %refs_0_.1, f32[8,32,128]{2,1,0:T(8,128)} %refs_1_.1, f32[8,32,128]{2,1,0:T(8,128)} %refs_2_.1, f32[32,128]{1,0:T(8,128)} %refs_3_.1, f32[32,128]{1,0:T(8,128)} %refs_4_.1, s32[32,128]{1,0:T(8,128)} %refs_5_.1, ...), custom_call_target="tpu_custom_call" | custom-call | tf_op jit(solution)/shard_map/pallas_call | solution.py:601
  41.8 1.6 %copy.15 = f32[8,32,128]{2,1,0:T(8,128)} copy(f32[8,32,128]{2,1,0:T(8,128)} %get-tuple-element.6) | data formatting | bytes 262144
  43.4 1.6 %copy.16 = f32[8,32,128]{2,1,0:T(8,128)} copy(f32[8,32,128]{2,1,0:T(8,128)} %get-tuple-element.7) | data formatting | bytes 262144
  44.9 1.6 %copy.17 = f32[8,32,128]{2,1,0:T(8,128)} copy(f32[8,32,128]{2,1,0:T(8,128)} %get-tuple-element.8) | data formatting | bytes 262144

commit v3 on v2

--- a/solution.py
+++ b/solution.py
@@ -199,7 +199,7 @@
 
 def fused_kernel(
     lat_count, lon_count, misfit_far, east_far, north_far, depth_far, drag_far, wet_far, table_in, love_far,
-    order_far, out_h, out_u, out_w, table, pack, rlon, rlat, rdepth, rdrag, rwet, coef, stepped, gath,
+    order_far, out, table, pack, rlon, rlat, rdepth, rdrag, rwet, coef, stepped, gath,
     forward_table, inverse_table, order_col, weights, spec_out, spec_in, syn_out, syn, pack2, rlon2,
     rw2, total, rh3, loading, own, depth_in, drag_in, wet_in, love_in, order_in, own_sem, table_sem, lat_send, lat_recv, lon_send, lon_recv, diag_send, diag_recv,
     g_send, g_recv, a_send, a_recv, b_send, b_recv, c_send, c_recv, w_send, w_recv, p_send, p_recv,
@@ -424,8 +424,7 @@
     coef[2] = 0.5 * wet_ext * depth_ext
     coef[3] = wet_ext
 
-    @pl.loop(0, fields)
-    def _(f):
+    def advance_field(f):
         keep, half, depth, wet = coef[0], coef[1], coef[2], coef[3]
         height = wet * assemble(misfit[f], rlat[0, f], rlon[0, 0], rlon[1, 0], f)
         east = wet * assemble(flow_east[f], rlat[1, f], rlon[0, 0], rlon[1, 0], f + fields)
@@ -438,18 +437,21 @@
         stepped[2, f] = north[:rows, :cols]
         gath[lon, pl.ds(pl.multiple_of(f * rows, rows), rows), :] = height.astype(jnp.bfloat16)
 
-    def lon_gather(ref, send, recv):
-        return [
-            remote(ref.at[lon], ref.at[lon], send.at[d - 1], recv.at[d - 1], lat, lax.rem(lon + d, lon_count))
-            for d in range(1, lon_count)
-        ]
+    halves = fields // 2
+    g_copies = []
+    for part in range(2):
+        pl.loop(part * halves, (part + 1) * halves)(advance_field)
+        span_rows = pl.ds(part * halves * rows, halves * rows)
+        for d in range(1, lon_count):
+            copy = remote(
+                gath.at[lon, span_rows], gath.at[lon, span_rows], g_send.at[part, d - 1],
+                g_recv.at[part, d - 1], lat, lax.rem(lon + d, lon_count),
+            )
+            copy.start()
+            g_copies.append(copy)
 
     def source(d):
         return lax.rem(lon + lon_count - d, lon_count)
-
-    g_copies = lon_gather(gath, g_send, g_recv)
-    for copy in g_copies:
-        copy.start()
 
     pack_edges(([stepped[k, f] for k in range(2) for f in range(fields)],), pack2)
 
@@ -473,6 +475,7 @@
     both = transform(lon)
     for d in range(1, lon_count):
         g_copies[d - 1].wait_recv()
+        g_copies[lon_count - 1 + d - 1].wait_recv()
         both = both + transform(source(d))
     spectra = (both[:block] + both[block:]).astype(jnp.bfloat16)
     for i in range(lat_count):
@@ -573,9 +576,9 @@
         east = assemble(stepped[1, f], none, rlon2[0], rlon2[1], f + fields)
         north = assemble(stepped[2, f], rw2[f], jnp.zeros((ext_rows, cols), jnp.float32), jnp.zeros((ext_rows, cols), jnp.float32), 0)
         height, east, north = step_on_tile(height, east, north, keep, half, depth)
-        out_h[f] = height[:rows, :cols]
-        out_u[f] = east[:rows, :cols]
-        out_w[f] = north[:rows, :cols]
+        out[0, f] = height[:rows, :cols]
+        out[1, f] = east[:rows, :cols]
+        out[2, f] = north[:rows, :cols]
 
     on_sides(lat_copies, wait_send, wait_send)
     on_sides(w_copies, wait_send, wait_send)
@@ -595,14 +598,14 @@
     block = lat_count * pair
     f32, b16 = jnp.float32, jnp.bfloat16
     ext_rows = rows + 2 * EDGE
-    tile = jax.ShapeDtypeStruct((fields, rows, cols), f32)
+    tiles = jax.ShapeDtypeStruct((3, fields, rows, cols), f32)
     vmem = pl.BlockSpec(memory_space=pltpu.VMEM)
     dma = pltpu.SemaphoreType.DMA
-    return pl.pallas_call(
+    stacked = pl.pallas_call(
         lambda *refs: fused_kernel(lat_count, lon_count, *refs),
-        out_shape=(tile, tile, tile),
+        out_shape=tiles,
         in_specs=[pl.BlockSpec(memory_space=pltpu.HBM)] * 9,
-        out_specs=(vmem, vmem, vmem),
+        out_specs=vmem,
         scratch_shapes=[
             pltpu.VMEM((slots, lats, used), b16),
             pltpu.VMEM((2, 2, rows, cols), f32),
@@ -637,7 +640,7 @@
             dma((8,)),
             dma,
             dma((2, 6)), dma((2, 6)), dma((2,)), dma((2,)), dma((4,)), dma((4,)),
-            dma((lon_count - 1,)), dma((lon_count - 1,)),
+            dma((2, lon_count - 1)), dma((2, lon_count - 1)),
             dma((lat_count - 1,)), dma((lat_count - 1,)), dma((lat_count - 1,)), dma((lat_count - 1,)),
             dma((lon_count - 1, lat_count)), dma((lon_count - 1, lat_count)),
             dma((2,)), dma((2,)), dma((2,)), dma((2,)), dma((2,)), dma((2,)),
@@ -649,6 +652,7 @@
         misfit, flow_east, flow_north, ocean_depth, drag_rate, wet_mask, legendre,
         love_factor.reshape(1, -1), assignment.reshape(1, -1),
     )
+    return stacked[0], stacked[1], stacked[2]
 
 
 def whole(*arrays):

time: 46.7 us -> 42.4 us (0.908)
  local copies, waits for them, and re-layouts: 4.7 us -> 1.78 us
  Pallas kernels: 41.2 us -> 39.8 us
    unnamed x3 -> x0, local copies, waits for them, and re-layouts: 4.7 us -> none
    squeeze x0 -> x1, local copies, waits for them, and re-layouts: none -> 1.78 us  [fused(): return (stacked[0], stacked[1], stacked[2])]
    pallas_call x1, Pallas kernels: 41.2 us -> 39.8 us  [fused(): pl.pallas_call(lambda *refs: fused_kernel(lat_count, lon_count, *refs), o...]
where the time goes in v3:
time: 42.4 us; the launch traced here: 42.2 us
  Pallas kernels  39.8 us (94%)
  local copies, waits for them, and re-layouts  1.78 us (4%)
  between operations  0.64 us (2%)
    pallas_call x1, Pallas kernels, fused(): pl.pallas_call(lambda *refs: fused_kernel(lat_count, lon_count, *refs), o...  39.8 us
    squeeze x1, local copies, waits for them, and re-layouts, fused(): return (stacked[0], stacked[1], stacked[2])  1.78 us

profile of v3, /device:TPU:1, one launch (start us, length us, event | category | flops | bytes accessed | tf_op | source)
XLA Modules:
  0.0 42.2 jit_solution(2027554723977344481)
XLA Ops:
  0.6 39.8 %shard_map.112 = f32[3,8,32,128]{3,2,1,0:T(8,128)} custom-call(f32[8,32,128]{2,1,0:T(8,128)} %refs_0_.1, f32[8,32,128]{2,1,0:T(8,128)} %refs_1_.1, f32[8,32,128]{2,1,0:T(8,128)} %refs_2_.1, f32[32,128]{1,0:T(8,128)} %refs_3_.1, f32[32,128]{1,0:T(8,128)} %refs_4_.1, s32[32,128]{1,0:T(8,128)} %refs_5_.1, bf16[8,256,1024]{2,1,0:T(8,128)(2,1)} %refs_6_.1, ...), custom_call_target="tpu_custom_call" | custom-call | tf_op jit(solution)/shard_map/pallas_call | solution.py:604
  40.5 1.8 %slice_bitcast_fusion = (f32[8,32,128]{2,1,0:T(8,128)}, f32[8,32,128]{2,1,0:T(8,128)}, f32[8,32,128]{2,1,0:T(8,128)}) fusion(f32[3,8,32,128]{3,2,1,0:T(8,128)} %shard_map.112), kind=kLoop, calls=%fused_computation | loop fusion | bytes 786432 | tf_op jit(solution)/shard_map/squeeze | solution.py:655
